TPU v7x, 768 devices: a whole 4x8x12 slice. The times are simulated.
768 devices in a mesh: replica: 48 (over z, y_hi), fsdp: 16 (over x, y_lo, core).
Axes of the slice: x: 4, y: 8 (y_hi: 4, y_lo: 2; y = y_hi * 2 + y_lo), z: 12, core: 2. Of those that a mesh axis runs over, the one named last changes fastest.
Arguments:
- activations: bfloat16 [48, 2048, 8192], P('replica', 'fsdp'), may hold values from -6 to 6
- grad_out: bfloat16 [48, 2048, 1024], P('replica', 'fsdp'), may hold values from -6 to 6
- local_weight: bfloat16 [48, 8192, 1024], P('replica', 'fsdp'), may hold values from -6 to 6
- anchor: float32 [8192, 1024], P('fsdp'), may hold values from -6 to 6
- momentum: float32 [8192, 256], P('fsdp'), may hold values from -6 to 6
- projection_key: int32 [2], replicated, may hold values from 0 to 1073741823
Outputs:
- new_anchor: float32 [8192, 1024], P('fsdp')
- new_momentum: float32 [8192, 256], P('fsdp')
All inputs are finite; a program needn't handle non-finite values.
Results may differ from a plain program's by a relative error of at most 0.0017.
Values may be sent and summed in bfloat16 or wider, within the bound.
No kernel may reach another device: no remote copies, remote signals or barrier semaphores. Data moves between devices by JAX's collectives and lax.ppermute only.
A program may use at most 32 MiB of HBM per device.

v0:
```python
import jax
import jax.numpy as jnp
from jax import lax
from jax.sharding import PartitionSpec as P

HIGH = lax.Precision.HIGHEST


def projection(words, rows, cols):
    k_index = lax.broadcasted_iota(jnp.int32, (rows, cols), 0)
    r_index = lax.broadcasted_iota(jnp.int32, (rows, cols), 1)
    hashed = words[0] + k_index * 668265261 + r_index * 374761393 + words[1] * 1103515245
    hashed = jnp.bitwise_xor(hashed, lax.shift_right_logical(hashed, jnp.int32(15)))
    hashed = hashed * 739982445
    hashed = jnp.bitwise_xor(hashed, lax.shift_right_logical(hashed, jnp.int32(12)))
    hashed = hashed * 695938361
    hashed = jnp.bitwise_xor(hashed, lax.shift_right_logical(hashed, jnp.int32(15)))
    level = jnp.bitwise_and(lax.shift_right_logical(hashed, jnp.int32(8)), 65535).astype(
        jnp.float32
    )
    return ((level + 0.5) / 65536.0 - 0.5) * (12.0 / float(cols)) ** 0.5


def on_device(activations, grad_out, local_weight, anchor, momentum, projection_key):
    inputs = activations[0]
    grads = grad_out[0]
    local = local_weight[0]
    width_k = grads.shape[1]
    rank_cols = momentum.shape[1]
    proj = projection(projection_key, width_k, rank_cols)
    replicas = lax.axis_size("replica")
    scale = float(inputs.shape[0] * lax.axis_size("fsdp")) ** (-0.5)
    drift = anchor - local.astype(jnp.float32)
    columns = lax.all_to_all(inputs, "fsdp", split_axis=1, concat_axis=0, tiled=True)
    weight_grad = lax.dot_general(
        columns,
        lax.all_gather(grads, "fsdp", axis=0, tiled=True),
        (((0,), (0,)), ((), ())),
        preferred_element_type=jnp.float32,
    )
    grad_part = jnp.dot(weight_grad, proj, precision=HIGH)
    local_term = jnp.dot(drift, proj, precision=HIGH) + scale * grad_part
    summed = lax.psum(local_term, "replica")
    compressed_mean = summed / replicas
    new_momentum = 0.9 * momentum + compressed_mean
    update = compressed_mean + 0.9 * new_momentum
    new_anchor = anchor - 0.7 * jnp.dot(update, proj.T, precision=HIGH)
    return (new_anchor, new_momentum)


def solution(mesh):
    placed = (
        P("replica", "fsdp", None),
        P("replica", "fsdp", None),
        P("replica", "fsdp", None),
        P("fsdp", None),
        P("fsdp", None),
        P(),
    )
    return jax.shard_map(
        on_device,
        mesh=mesh,
        in_specs=placed,
        out_specs=(P("fsdp", None), P("fsdp", None)),
        check_vma=False,
    )
```

profile of v0, /device:TPU:240, one launch (start us, length us, event | category | flops | bytes accessed | tf_op | source)
XLA Modules:
  0.0 554.5 jit_solution(1428324686451430451)
XLA Ops:
  7.2 0.0 all-gather.3.cloned.1.call-start
  7.2 0.7 all-gather.3.cloned.1.call-update
  7.9 4.1 copy.8
  12.0 0.0 copy-start.2
  12.0 0.0 copy-start.4
  12.0 4.6 all-to-all-start
  16.6 0.0 all-reduce.2.cloned.1.call-start
  16.7 0.0 copy-done.2
  16.7 0.6 fusion.54
  18.0 0.7 multiply_add_fusion.1
  18.7 0.0 copy-done.4
  18.7 4.9 fusion.2
  23.6 28.0 %all-to-all-done = bf16[128,16,512]{0,2,1:T(8,128)(2,1)S(1)} async-done(((bf16[128,16,512]{0,2,1:T(8,128)(2,1)}), bf16[128,16,512]{0,2,1:T(8,128)(2,1)S(1)}, u32[]{:S(2)}, u32[]{:S(2)}) %all-to-all-start) | async-done | bytes 2097184 | tf_op jit(solution)/shard_map/all_to_all | solution.py:34
  51.5 2.6 copy.9
  54.1 13.9 %all-gather.3.cloned.1.call-done = bf16[1,2048,1024]{2,1,0:T(8,128)(2,1)} async-done(((bf16[1,128,1024]{2,1,0:T(8,128)(2,1)}), bf16[1,2048,1024]{2,1,0:T(8,128)(2,1)}) %all-gather.3.cloned.1.call-update) | async-done | bytes 4194320 | tf_op jit(solution)/shard_map/all_gather | solution.py:37
  68.0 0.0 copy-start.5
  68.0 5.2 fusion
  73.2 0.0 copy-done.5
  73.3 0.0 copy-start
  73.3 3.2 fusion.3
  76.5 0.0 copy-start.3
  76.5 0.0 all-reduce.2.cloned.1.call-update
  76.5 464.7 %all-reduce.2.cloned.1.call-done = f32[512,256]{1,0:T(8,128)} async-done(((f32[512,256]{1,0:T(8,128)}), f32[512,256]{1,0:T(8,128)}) %all-reduce.2.cloned.1.call-update) | async-done | bytes 524304 | tf_op jit(solution)/shard_map/psum | solution.py:43
  541.3 0.0 copy-done
  541.3 1.1 multiply_add_fusion
  542.4 0.0 copy-done.3
  542.4 0.0 copy-start.1
  542.4 5.2 multiply_subtract_fusion
  547.6 0.0 copy-done.1
  (1 shorter events, 0.0 us)
Async XLA Ops:
  7.2 60.9 %all-gather.3.cloned.1.call-start = ((), (), s32[]{:S(2)}) async-start(), calls=%async_computation.2 | async-start | bytes 4456448 | tf_op jit(solution)/shard_map/all_gather | solution.py:37
  12.0 4.7 copy-start.2
  12.0 6.7 %copy-start.4 = (bf16[1,512,1024]{2,1,0:T(8,128)(2,1)S(1)}, bf16[1,512,1024]{2,1,0:T(8,128)(2,1)}, u32[]{:S(2)}) copy-start(bf16[1,512,1024]{2,1,0:T(8,128)(2,1)} %param.8) | copy-start | bytes 3145732
  12.0 39.6 %all-to-all-start = ((bf16[128,16,512]{0,2,1:T(8,128)(2,1)}), bf16[128,16,512]{0,2,1:T(8,128)(2,1)S(1)}, u32[]{:S(2)}, u32[]{:S(2)}) async-start(bf16[128,16,512]{0,2,1:T(8,128)(2,1)} %bitcast.17), calls=%async_computation | async-start | bytes 4194304 | tf_op jit(solution)/shard_map/all_to_all | solution.py:34
  16.6 524.6 %all-reduce.2.cloned.1.call-start = ((), (), s32[]{:S(2)}) async-start(), calls=%async_computation.1 | async-start | bytes 1048576 | tf_op jit(solution)/shard_map/psum | solution.py:43
  68.0 5.2 copy-start.5
  73.3 468.0 %copy-start = (f32[512,256]{1,0:T(8,128)S(1)}, f32[512,256]{1,0:T(8,128)}, u32[]{:S(2)}) copy-start(f32[512,256]{1,0:T(8,128)} %param.10) | copy-start | bytes 1572868
  76.5 465.9 %copy-start.3 = (f32[512,1024]{1,0:T(8,128)S(1)}, f32[512,1024]{1,0:T(8,128)}, u32[]{:S(2)}) copy-start(f32[512,1024]{1,0:T(8,128)} %param.9) | copy-start | bytes 6291460
  542.4 5.2 copy-start.1
Sparse Core Ops, SparseCore 0:
  10.4 57.5 all-gather.2
  76.6 464.5 all-reduce.1
where the time goes:
time: 555 us; the launch traced here: 554 us
  waiting for transfers between devices  507 us (91%)
  matrix products  18.5 us (3%)
  between operations  14.8 us (3%)
  local copies, waits for them, and re-layouts  7.33 us (1%)
    psum x1, waiting for transfers between devices, on_device(): summed = lax.psum(local_term, 'replica')  465 us
    all_to_all x1, waiting for transfers between devices, on_device(): lax.all_to_all(inputs, 'fsdp', split_axis=1, concat_axis=0, tiled=True)  28 us
    all_gather x1, waiting for transfers between devices, on_device(): lax.all_gather(grads, 'fsdp', axis=0, tiled=True)  13.9 us
  transfers between devices with their start and end apart: 3, of which 3 were waited for; matrix products, arithmetic and copies ran while one was open for 2% of the time, Pallas kernels for 0%

commit v1 on v0

v1 whole, which is shorter than its diff:
```python
import jax
import jax.numpy as jnp
from jax import lax
from jax.sharding import PartitionSpec as P

F32 = jnp.float32
BF16 = jnp.bfloat16


def projection_parts(words, rows, cols):
    k_index = lax.broadcasted_iota(jnp.int32, (rows, cols), 0)
    r_index = lax.broadcasted_iota(jnp.int32, (rows, cols), 1)
    hashed = words[0] + k_index * 668265261 + r_index * 374761393 + words[1] * 1103515245
    hashed = jnp.bitwise_xor(hashed, lax.shift_right_logical(hashed, jnp.int32(15)))
    hashed = hashed * 739982445
    hashed = jnp.bitwise_xor(hashed, lax.shift_right_logical(hashed, jnp.int32(12)))
    hashed = hashed * 695938361
    hashed = jnp.bitwise_xor(hashed, lax.shift_right_logical(hashed, jnp.int32(15)))
    high = jnp.bitwise_and(lax.shift_right_logical(hashed, jnp.int32(16)), 255).astype(F32)
    low = jnp.bitwise_and(lax.shift_right_logical(hashed, jnp.int32(8)), 255).astype(F32)
    return ((high - 127.5) * 256.0).astype(BF16), (low - 127.5).astype(BF16)


def halves(x):
    top = lax.reduce_precision(x, 8, 7)
    return top.astype(BF16), (x - top).astype(BF16)


def mm(a, b, dims=(((1,), (0,)), ((), ()))):
    return lax.dot_general(a, b, dims, preferred_element_type=F32)


def groups(z_of, y_of):
    return [[z * 4 + y for z in zs for y in ys] for zs in z_of for ys in y_of]


def on_device(activations, grad_out, local_weight, anchor, momentum, projection_key):
    inputs, grads, local = activations[0], grad_out[0], local_weight[0]
    tokens, width = inputs.shape
    width_k, rank = grads.shape[1], momentum.shape[1]
    rows = anchor.shape[0]
    replicas, shards = lax.axis_size("replica"), lax.axis_size("fsdp")
    unit = (12.0 / float(rank)) ** 0.5 / 65536.0
    scale = float(tokens * shards) ** (-0.5)
    chips = shards // 2
    core = lax.rem(lax.axis_index("fsdp"), 2)
    swap = [(i, i ^ 1) for i in range(shards)]
    same_core = [[2 * i + c for i in range(chips)] for c in range(2)]
    near = groups([range(4 * h, 4 * h + 4) for h in range(3)], [range(4)])
    far = groups([range(l, 12, 4) for l in range(4)], [[y] for y in range(4)])

    by_core = inputs.reshape(tokens, chips, 2, rows)
    keep = lax.dynamic_index_in_dim(by_core, core, 2, keepdims=False)
    give = lax.dynamic_index_in_dim(by_core, 1 - core, 2, keepdims=False)
    got = lax.ppermute(give, "fsdp", swap)
    got_grads = lax.ppermute(grads, "fsdp", swap)

    part_a, part_b = projection_parts(projection_key, width_k, rank)
    part_a, part_b = lax.optimization_barrier((part_a, part_b))

    def chip_half(acts, gs):
        projected = unit * (mm(gs, part_a) + mm(gs, part_b))
        top, rest = halves(projected)
        cols = acts.reshape(tokens, chips * rows)
        dims = (((0,), (0,)), ((), ()))
        return mm(cols, top, dims) + mm(cols, rest, dims)

    partial = (chip_half(keep, grads) + chip_half(got, got_grads)).astype(BF16)
    landed = lax.all_to_all(partial.reshape(chips, rows, rank), "fsdp", 0, 0, tiled=True, axis_index_groups=same_core)
    local_term = unit * (mm(local, part_a) + mm(local, part_b))
    mine = scale * jnp.sum(landed.astype(F32), axis=0) - local_term

    pieces = lax.all_to_all(mine.reshape(16, rows // 16, rank), "replica", 0, 0, tiled=True, axis_index_groups=near)
    piece = jnp.sum(pieces, axis=0)
    thirds = lax.all_to_all(jnp.broadcast_to(piece[None], (3,) + piece.shape), "replica", 0, 0, tiled=True, axis_index_groups=far)
    piece = jnp.sum(thirds, axis=0)
    spread = lax.all_to_all(jnp.broadcast_to(piece[None], (16,) + piece.shape), "replica", 0, 0, tiled=True, axis_index_groups=near)

    top, rest = halves(anchor)
    anchor_term = unit * (mm(top, part_a) + mm(top, part_b) + mm(rest, part_a))
    compressed_mean = anchor_term + spread.reshape(rows, rank) / replicas
    new_momentum = 0.9 * momentum + compressed_mean
    update = compressed_mean + 0.9 * new_momentum
    top, rest = halves(update)
    dims = (((1,), (1,)), ((), ()))
    product = mm(top, part_a, dims) + mm(top, part_b, dims) + mm(rest, part_a, dims)
    new_anchor = anchor - (0.7 * unit) * product
    return (new_anchor, new_momentum)


def solution(mesh):
    placed = (
        P("replica", "fsdp", None),
        P("replica", "fsdp", None),
        P("replica", "fsdp", None),
        P("fsdp", None),
        P("fsdp", None),
        P(),
    )
    return jax.shard_map(
        on_device,
        mesh=mesh,
        in_specs=placed,
        out_specs=(P("fsdp", None), P("fsdp", None)),
        check_vma=False,
    )
```

time: 555 us -> 147 us (0.26)
  the two profiles are of different devices: /device:TPU:240 before, /device:TPU:8 now
where the time goes in v1:
time: 147 us; the launch traced here: 146 us
  blocking collectives  40.7 us (28%)
  waiting for transfers between devices  36.1 us (25%)
  starting transfers between devices  22.2 us (15%)
  matrix products  21.5 us (15%)
  local copies, waits for them, and re-layouts  18 us (12%)
  other arithmetic  6.45 us (4%)
  between operations  1.49 us (1%)
    all_to_all x1, waiting for transfers between devices, on_device(): lax.all_to_all(partial.reshape(chips, rows, rank), 'fsdp', 0, 0, tiled=Tr...  25.1 us
    dot_general x16, matrix products, mm(): return lax.dot_general(a, b, dims, preferred_element_type=F32)  21.5 us
    all_to_all x1, blocking collectives, on_device(): lax.all_to_all(mine.reshape(16, rows // 16, rank), 'replica', 0, 0, tiled...  20.9 us
    all_to_all x1, blocking collectives, on_device(): lax.all_to_all(jnp.broadcast_to(piece[None], (3,) + piece.shape), 'replic...  19.8 us
    all_to_all x1, starting transfers between devices, on_device(): lax.all_to_all(partial.reshape(chips, rows, rank), 'fsdp', 0, 0, tiled=Tr...  13.7 us
    all_to_all x1, waiting for transfers between devices, on_device(): lax.all_to_all(jnp.broadcast_to(piece[None], (16,) + piece.shape), 'repli...  11 us
    unnamed x24, local copies, waits for them, and re-layouts  8.7 us
    dynamic_slice x2, local copies, waits for them, and re-layouts, on_device(): give = lax.dynamic_index_in_dim(by_core, 1 - core, 2, keepdims=False)  5.38 us
  transfers between devices with their start and end apart: 4, of which 2 were waited for; matrix products, arithmetic and copies ran while one was open for 8% of the time, Pallas kernels for 0%

profile of v1, /device:TPU:8, one launch (start us, length us, event | category | flops | bytes accessed | tf_op | source)
XLA Modules:
  0.0 146.4 jit_solution(5544297256546666686)
XLA Ops:
  0.6 0.0 copy-start
  0.7 4.2 %copy.33 = bf16[1,128,8192]{1,2,0:T(8,128)(2,1)} copy(bf16[1,128,8192]{2,1,0:T(8,128)(2,1)} %param.6) | data formatting | bytes 4194304 | tf_op args[0]
  4.8 2.7 %constant_dynamic-slice_fusion = (bf16[128,8,1,512]{0,3,2,1:T(8,128)(2,1)}, bf16[128,8,1,512]{0,3,2,1:T(8,128)(2,1)S(1)}) fusion(bf16[128,8,2,512]{0,3,2,1:T(8,128)(2,1)} %bitcast.54, s32[]{:T(128)S(6)} %select_n.8, s32[]{:T(128)S(6)} %select_n.7), kind=kLoop, calls=%fused_computation.51 | loop fusion | bytes 4194312 | tf_op jit(solution)/shard_map/jit(dynamic_index_in_dim)/dynamic_slice | solution.py:54
  7.5 0.0 copy-start.8
  7.5 0.0 copy-start.9
  7.5 2.7 %copy.34 = bf16[128,8,1,512]{3,1,0,2:T(8,128)(2,1)} copy(bf16[128,8,1,512]{0,3,2,1:T(8,128)(2,1)} %get-tuple-element.16) | data formatting | bytes 2097152 | tf_op jit(solution)/shard_map/jit(dynamic_index_in_dim)/dynamic_slice | solution.py:54
  10.2 1.9 %collective-permute-start = (bf16[128,8,512]{2,1,0:T(8,128)(2,1)}, bf16[128,8,512]{2,1,0:T(8,128)(2,1)S(1)}, u32[]{:S(2)}, u32[]{:S(2)}) collective-permute-start(bf16[128,8,512]{2,1,0:T(8,128)(2,1)} %bitcast.58), channel_id=1, source_target_pairs={{0,1},{1,0},{2,3},{3,2},{4,5},{5,4},{6,7},{7,6},{8,9},{9,8},{10,11... | collective-permute-start | bytes 3145736 | tf_op jit(solution)/shard_map/ppermute | solution.py:55
  12.1 0.0 copy-done.8
  12.1 2.4 %collective-permute-start.1 = (bf16[128,1024]{1,0:T(8,128)(2,1)S(1)}, bf16[128,1024]{1,0:T(8,128)(2,1)S(1)}, u32[]{:S(2)}, u32[]{:S(2)}) collective-permute-start(bf16[128,1024]{1,0:T(8,128)(2,1)S(1)} %bitcast.60), channel_id=1, source_target_pairs={{0,1},{1,0},{2,3},{3,2},{4,5},{5,4},{6,7},{7,6},{8,9},{9,8},{10,11... | collective-permute-start | bytes 786440 | tf_op jit(solution)/shard_map/ppermute | solution.py:56
  14.5 0.0 copy-done.9
  14.6 0.6 fusion.32
  15.2 0.6 multiply_add_fusion.3
  16.5 0.8 add_convert_fusion
  17.2 0.0 copy-start.2
  17.2 0.0 copy-start.4
  17.3 0.3 fusion.29
  17.6 0.3 fusion.12
  17.9 0.7 fusion.27
  18.6 0.7 convolution_add_fusion.1
  19.4 0.0 collective-permute-done.1
  19.4 0.3 fusion.33
  19.7 0.3 fusion.10
  20.1 0.0 collective-permute-done
  20.1 0.4 copy.41
  20.5 0.7 fusion.24
  21.2 2.1 %fusion.1 = bf16[4096,256]{1,0:T(8,128)(2,1)} fusion(f32[4096,256]{1,0:T(8,128)S(1)} %convolution_add_fusion.1, f32[4096,256]{1,0:T(8,128)S(1)} %fusion.24, bf16[128,4096]{1,0:T(8,128)(2,1)S(1)} %bitcast.53, f32[128,256]{0,1:T(8,128)S(1)} %fusion.10), kind=kOutput, calls=%fused_computation.3 | convolution fusion | flops 271646720 | bytes 11665408 | tf_op jit(solution)/shard_map/dot_general | solution.py:30
  23.3 13.7 %all-to-all-start = ((bf16[8,512,256]{2,1,0:T(8,128)(2,1)}), bf16[8,512,256]{2,1,0:T(8,128)(2,1)}, u32[]{:S(2)}, u32[]{:S(2)}) async-start(bf16[8,512,256]{2,1,0:T(8,128)(2,1)} %bitcast.55), calls=%async_computation | async-start | bytes 4194304 | tf_op jit(solution)/shard_map/all_to_all | solution.py:69
  36.9 0.0 copy-done.2
  36.9 0.0 copy-done
  36.9 1.3 fusion.17
  38.2 0.0 copy-start.7
  38.2 25.1 %all-to-all-done = bf16[8,512,256]{2,1,0:T(8,128)(2,1)} async-done(((bf16[8,512,256]{2,1,0:T(8,128)(2,1)}), bf16[8,512,256]{2,1,0:T(8,128)(2,1)}, u32[]{:S(2)}, u32[]{:S(2)}) %all-to-all-start) | async-done | bytes 2097184 | tf_op jit(solution)/shard_map/all_to_all | solution.py:69
  63.3 1.9 %convert_reduce_fusion = f32[512,256]{1,0:T(8,128)S(1)} fusion(bf16[8,512,256]{2,1,0:T(8,128)(2,1)} %all-to-all-done), kind=kLoop, calls=%fused_computation.4 | loop fusion | flops 1966080 | bytes 2621440 | tf_op jit(solution)/shard_map/reduce_sum | solution.py:71
  65.2 0.2 copy.35
  65.4 0.0 copy-done.4
  65.4 0.0 copy-done.7
  65.4 0.5 fusion.7
  66.0 0.2 copy.36
  66.2 20.9 %all_to_all.20 = f32[16,32,256]{2,1,0:T(8,128)} all-to-all(f32[16,32,256]{2,1,0:T(8,128)S(1)} %bitcast.56), channel_id=1, replica_groups={{0,16,32,48,64,80,96,112,128,144,160,176,192,208,224,240},{256,272,288,..., dimensions={0} | all-to-all | bytes 1048576 | tf_op jit(solution)/shard_map/all_to_all | solution.py:73
  87.1 0.0 copy-start.1
  87.1 1.2 reduce_sum.28
  88.3 19.8 %all_to_all.21 = f32[3,32,256]{2,1,0:T(8,128)S(1)} all-to-all(f32[3,32,256]{2,1,0:T(8,128)S(1)} %broadcast_in_dim.4), channel_id=1, replica_groups={{0,256,512},{16,272,528},{32,288,544},{48,304,560},{64,320,576},{80,336..., dimensions={0} | all-to-all | bytes 196608 | tf_op jit(solution)/shard_map/all_to_all | solution.py:75
  108.1 0.8 broadcast_in_dim.5
  109.0 4.2 %all-to-all-start.3 = ((f32[16,32,256]{2,1,0:T(8,128)}), f32[16,32,256]{2,1,0:T(8,128)}, u32[]{:S(2)}, u32[]{:S(2)}) async-start(f32[16,32,256]{2,1,0:T(8,128)} %broadcast_in_dim.5), calls=%async_computation.3 | async-start | bytes 1048576 | tf_op jit(solution)/shard_map/all_to_all | solution.py:77
  113.2 2.1 %copy.38 = f32[512,256]{0,1:T(8,128)} copy(f32[512,256]{1,0:T(8,128)} %param.10) | data formatting | bytes 1048576 | tf_op args[4]
  115.3 0.0 copy-done.1
  115.3 0.0 copy-start.5
  115.3 1.6 %fusion.20 = f32[256,512]{1,0:T(8,128)S(1)} fusion(bf16[1024,256]{1,0:T(8,128)(2,1)} %copy-done.2, f32[512,1024]{1,0:T(8,128)S(1)} %copy-done.1), kind=kOutput, calls=%fused_computation.39 | convolution fusion | flops 269484032 | bytes 3145728 | tf_op jit(solution)/shard_map/dot_general | solution.py:30
  116.9 0.0 copy-done.5
  116.9 1.3 fusion.3
  118.2 11.0 %all-to-all-done.3 = f32[16,32,256]{2,1,0:T(8,128)} async-done(((f32[16,32,256]{2,1,0:T(8,128)}), f32[16,32,256]{2,1,0:T(8,128)}, u32[]{:S(2)}, u32[]{:S(2)}) %all-to-all-start.3) | async-done | bytes 524320 | tf_op jit(solution)/shard_map/all_to_all | solution.py:77
  129.1 1.9 %broadcast_multiply_fusion = f32[16,32,256]{2,1,0:T(8,128)} fusion(f32[16,32,256]{2,1,0:T(8,128)} %all-to-all-done.3), kind=kLoop, calls=%fused_computation.40 | loop fusion | flops 131072 | bytes 1048576 | tf_op jit(solution)/shard_map/div | solution.py:81
  131.0 2.0 %copy.37 = f32[512,256]{0,1:T(8,128)} copy(f32[512,256]{1,0:T(8,128)} %bitcast.57) | data formatting | bytes 1048576 | tf_op jit(solution)/shard_map/div | solution.py:81
  133.1 0.0 copy-start.6
  133.1 3.1 %multiply_add_fusion.1 = (f32[512,256]{0,1:T(8,128)}, bf16[512,256]{0,1:T(8,128)(2,1)S(1)}, f32[512,256]{0,1:T(8,128)}) fusion(f32[512,256]{0,1:T(8,128)} %copy.38, f32[512,256]{0,1:T(8,128)} %copy.37, f32[512,256]{0,1:T(8,128)} %fusion.3, bf16[1024,256]{1,0:T(8,128)(2,1)} %copy-done.2, f32[512,1024]{1,0:T(8,128)S(1)} %copy-done.1), kind=kOutput, calls=%fused_computation.38 | convolution fusion | flops 271187968 | bytes 5505024 | tf_op jit(solution)/shard_map/dot_general | solution.py:30
  136.2 0.0 copy-start.3
  136.2 0.0 copy-done.6
  136.2 1.8 %fusion.35 = f32[512,1024]{1,0:T(8,128)} fusion(bf16[512,256]{0,1:T(8,128)(2,1)S(1)} %get-tuple-element.19, bf16[1024,256]{1,0:T(8,128)(2,1)S(1)} %copy-done.6), kind=kOutput, calls=%fused_computation.60 | convolution fusion | flops 268435456 | bytes 2883584 | tf_op jit(solution)/shard_map/dot_general | solution.py:30
  138.0 0.0 copy-done.3
  138.0 1.8 %fusion.34 = f32[512,1024]{1,0:T(8,128)} fusion(bf16[512,256]{0,1:T(8,128)(2,1)S(1)} %get-tuple-element.19, bf16[1024,256]{1,0:T(8,128)(2,1)S(1)} %copy-done.3), kind=kOutput, calls=%fused_computation.59 | convolution fusion | flops 268435456 | bytes 2883584 | tf_op jit(solution)/shard_map/dot_general | solution.py:30
  139.8 2.0 %copy.39 = f32[512,256]{1,0:T(8,128)} copy(f32[512,256]{0,1:T(8,128)} %get-tuple-element.18) | data formatting | bytes 1048576
  141.9 4.6 %multiply_subtract_fusion = f32[512,1024]{1,0:T(8,128)} fusion(f32[512,1024]{1,0:T(8,128)S(1)} %copy-done.1, f32[512,1024]{1,0:T(8,128)} %fusion.34, f32[512,1024]{1,0:T(8,128)} %fusion.35, bf16[1024,256]{1,0:T(8,128)(2,1)} %copy-done.2, f32[512,256]{0,1:T(8,128)} %get-tuple-element.24, f32[512,256]{0,1:T(8,128)} %copy.38), kind=kOutput, calls=%fused_computation.8 | convolution fusion | flops 271450112 | bytes 9961472 | tf_op jit(solution)/shard_map/dot_general | solution.py:30
  (3 shorter events, 0.0 us)
Async XLA Ops:
  0.6 36.3 %copy-start = (bf16[1,512,1024]{2,1,0:T(8,128)(2,1)S(1)}, bf16[1,512,1024]{2,1,0:T(8,128)(2,1)}, u32[]{:S(2)}) copy-start(bf16[1,512,1024]{2,1,0:T(8,128)(2,1)} %param.8) | copy-start | bytes 3145732
  7.5 4.6 %copy-start.8 = (bf16[1,128,1024]{2,1,0:T(8,128)(2,1)S(1)}, bf16[1,128,1024]{2,1,0:T(8,128)(2,1)}, u32[]{:S(2)}) copy-start(bf16[1,128,1024]{2,1,0:T(8,128)(2,1)} %param.7) | copy-start | bytes 786436
  7.5 7.0 %copy-start.9 = (s32[2]{0:T(128)S(1)}, s32[2]{0:T(128)}, u32[]{:S(2)}) copy-start(s32[2]{0:T(128)} %param.11) | copy-start | bytes 28
  10.2 9.9 %collective-permute-start = (bf16[128,8,512]{2,1,0:T(8,128)(2,1)}, bf16[128,8,512]{2,1,0:T(8,128)(2,1)S(1)}, u32[]{:S(2)}, u32[]{:S(2)}) collective-permute-start(bf16[128,8,512]{2,1,0:T(8,128)(2,1)} %bitcast.58), channel_id=1, source_target_pairs={{0,1},{1,0},{2,3},{3,2},{4,5},{5,4},{6,7},{7,6},{8,9},{9,8},{10,11... | collective-permute-start | bytes 3145736 | tf_op jit(solution)/shard_map/ppermute | solution.py:55
  12.1 7.2 %collective-permute-start.1 = (bf16[128,1024]{1,0:T(8,128)(2,1)S(1)}, bf16[128,1024]{1,0:T(8,128)(2,1)S(1)}, u32[]{:S(2)}, u32[]{:S(2)}) collective-permute-start(bf16[128,1024]{1,0:T(8,128)(2,1)S(1)} %bitcast.60), channel_id=1, source_target_pairs={{0,1},{1,0},{2,3},{3,2},{4,5},{5,4},{6,7},{7,6},{8,9},{9,8},{10,11... | collective-permute-start | bytes 786440 | tf_op jit(solution)/shard_map/ppermute | solution.py:56
  17.2 19.7 %copy-start.2 = (bf16[1024,256]{1,0:T(8,128)(2,1)}, bf16[1024,256]{1,0:T(8,128)(2,1)S(1)}, u32[]{:S(2)}) copy-start(bf16[1024,256]{1,0:T(8,128)(2,1)S(1)} %get-tuple-element.4) | copy-start | bytes 1572868
  17.2 48.2 %copy-start.4 = (bf16[1024,256]{1,0:T(8,128)(2,1)}, bf16[1024,256]{1,0:T(8,128)(2,1)S(1)}, u32[]{:S(2)}) copy-start(bf16[1024,256]{1,0:T(8,128)(2,1)S(1)} %get-tuple-element.5) | copy-start | bytes 1572868
  23.3 40.0 %all-to-all-start = ((bf16[8,512,256]{2,1,0:T(8,128)(2,1)}), bf16[8,512,256]{2,1,0:T(8,128)(2,1)}, u32[]{:S(2)}, u32[]{:S(2)}) async-start(bf16[8,512,256]{2,1,0:T(8,128)(2,1)} %bitcast.55), calls=%async_computation | async-start | bytes 4194304 | tf_op jit(solution)/shard_map/all_to_all | solution.py:69
  38.2 27.2 %copy-start.7 = (f32[256,512]{1,0:T(8,128)S(1)}, f32[256,512]{1,0:T(8,128)}, u32[]{:S(2)}) copy-start(f32[256,512]{1,0:T(8,128)} %fusion.17) | copy-start | bytes 1572868
  87.1 28.2 %copy-start.1 = (f32[512,1024]{1,0:T(8,128)S(1)}, f32[512,1024]{1,0:T(8,128)}, u32[]{:S(2)}) copy-start(f32[512,1024]{1,0:T(8,128)} %param.9) | copy-start | bytes 6291460
  109.0 20.2 %all-to-all-start.3 = ((f32[16,32,256]{2,1,0:T(8,128)}), f32[16,32,256]{2,1,0:T(8,128)}, u32[]{:S(2)}, u32[]{:S(2)}) async-start(f32[16,32,256]{2,1,0:T(8,128)} %broadcast_in_dim.5), calls=%async_computation.3 | async-start | bytes 1048576 | tf_op jit(solution)/shard_map/all_to_all | solution.py:77
  115.3 1.6 %copy-start.5 = (bf16[1024,256]{1,0:T(8,128)(2,1)S(1)}, bf16[1024,256]{1,0:T(8,128)(2,1)}, u32[]{:S(2)}) copy-start(bf16[1024,256]{1,0:T(8,128)(2,1)} %copy-done.4) | copy-start | bytes 1572868
  133.1 3.1 %copy-start.6 = (bf16[1024,256]{1,0:T(8,128)(2,1)S(1)}, bf16[1024,256]{1,0:T(8,128)(2,1)}, u32[]{:S(2)}) copy-start(bf16[1024,256]{1,0:T(8,128)(2,1)} %copy-done.4) | copy-start | bytes 1572868
  136.2 1.8 %copy-start.3 = (bf16[1024,256]{1,0:T(8,128)(2,1)S(1)}, bf16[1024,256]{1,0:T(8,128)(2,1)}, u32[]{:S(2)}) copy-start(bf16[1024,256]{1,0:T(8,128)(2,1)} %copy-done.2) | copy-start | bytes 1572868

commit v2 on v1

v2 whole, which is shorter than its diff:
```python
import functools

import jax
import jax.numpy as jnp
from jax import lax
from jax.experimental import pallas as pl
from jax.experimental.pallas import tpu as pltpu
from jax.sharding import PartitionSpec as P

F32 = jnp.float32
BF16 = jnp.bfloat16
NN = (((1,), (0,)), ((), ()))
NT = (((1,), (1,)), ((), ()))


def mm(a, b, dims=NN):
    return lax.dot_general(a, b, dims, preferred_element_type=F32)


def split(x):
    top = x.astype(BF16)
    return top, (x - top.astype(F32)).astype(BF16)


def cost(flops, bytes_accessed):
    return pl.CostEstimate(flops=flops, bytes_accessed=bytes_accessed, transcendentals=0)


def front_kernel(factor, key_ref, grads_ref, a_ref, b_ref, top_ref, rest_ref):
    rank, width_k = a_ref.shape
    step = 256
    start = key_ref[0] + key_ref[1] * 1103515245
    r_index = lax.broadcasted_iota(jnp.int32, (rank, step), 0) * 374761393
    k_index = lax.broadcasted_iota(jnp.int32, (rank, step), 1) * 668265261
    base = r_index + k_index
    total = jnp.zeros((rank, grads_ref.shape[0]), F32)
    for k in range(0, width_k, step):
        shift = (k * 668265261 + 2**31) % 2**32 - 2**31
        hashed = base + (start + jnp.int32(shift))
        hashed = jnp.bitwise_xor(hashed, lax.shift_right_logical(hashed, jnp.int32(15)))
        hashed = hashed * 739982445
        hashed = jnp.bitwise_xor(hashed, lax.shift_right_logical(hashed, jnp.int32(12)))
        hashed = hashed * 695938361
        hashed = jnp.bitwise_xor(hashed, lax.shift_right_logical(hashed, jnp.int32(15)))
        high = jnp.bitwise_and(lax.shift_right_logical(hashed, jnp.int32(16)), 255).astype(F32)
        low = jnp.bitwise_and(lax.shift_right_logical(hashed, jnp.int32(8)), 255).astype(F32)
        part_a = ((high - 127.5) * 256.0).astype(BF16)
        part_b = (low - 127.5).astype(BF16)
        a_ref[:, k : k + step] = part_a
        b_ref[:, k : k + step] = part_b
        block = grads_ref[:, k : k + step]
        total += mm(part_a, block, NT) + mm(part_b, block, NT)
    top_ref[...], rest_ref[...] = split(factor * total)


def partial_kernel(factor, core_ref, own_ref, got_ref, gg_ref, a_ref, b_ref, top_ref, rest_ref, out_ref, tops, rests):
    tokens = own_ref.shape[0]

    @pl.when(pl.program_id(0) == 0)
    def _():
        other = factor * (mm(a_ref[...], gg_ref[...], NT) + mm(b_ref[...], gg_ref[...], NT))
        top, rest = split(other)
        tops[:, :tokens] = top_ref[...]
        tops[:, tokens:] = top
        rests[:, :tokens] = rest_ref[...]
        rests[:, tokens:] = rest

    acts = jnp.concatenate([own_ref[...], got_ref[...]], axis=0)
    out_ref[0] = (mm(tops[...], acts) + mm(rests[...], acts)).astype(BF16)


def side_kernel(unit, local_ref, anchor_ref, momentum_ref, a_ref, b_ref, local_term_ref, base_momentum_ref, base_anchor_ref):
    part_a, part_b = a_ref[...], b_ref[...]
    local = local_ref[...]
    local_term_ref[...] = unit * (mm(part_a, local, NT) + mm(part_b, local, NT))
    anchor = anchor_ref[...]
    top, rest = split(anchor)
    anchor_term = unit * (mm(top, part_a, NT) + mm(top, part_b, NT) + mm(rest, part_a, NT))
    base = 0.9 * momentum_ref[...] + anchor_term
    base_momentum_ref[...] = base
    top, rest = split(anchor_term + 0.9 * base)
    base_anchor_ref[...] = anchor - (0.7 * unit) * (mm(top, part_a) + mm(top, part_b) + mm(rest, part_a))


def last_kernel(unit, mean_ref, base_momentum_ref, base_anchor_ref, a_ref, b_ref, new_anchor_ref, new_momentum_ref):
    mean = mean_ref[...].astype(F32).T
    new_momentum_ref[...] = base_momentum_ref[...] + mean
    narrow = mean.astype(BF16)
    product = mm(narrow, a_ref[...]) + mm(narrow, b_ref[...])
    new_anchor_ref[...] = base_anchor_ref[...] - (0.7 * 1.9 * unit) * product


def limit(mib):
    return pltpu.CompilerParams(vmem_limit_bytes=mib << 20)


def total(x):
    return lax.reduce_precision(jnp.sum(x.astype(F32), axis=0), 8, 7).astype(BF16)


def groups(z_of, y_of):
    return [[z * 4 + y for z in zs for y in ys] for zs in z_of for ys in y_of]


def on_device(activations, grad_out, local_weight, anchor, momentum, projection_key):
    inputs, grads, local = activations[0], grad_out[0], local_weight[0]
    tokens, width = inputs.shape
    width_k, rank = grads.shape[1], momentum.shape[1]
    rows = anchor.shape[0]
    replicas, shards = lax.axis_size("replica"), lax.axis_size("fsdp")
    unit = (12.0 / float(rank)) ** 0.5 / 65536.0
    factor = unit * float(tokens * shards) ** (-0.5)
    chips = shards // 2
    core = lax.rem(lax.axis_index("fsdp"), 2).reshape(1)
    swap = [(i, i ^ 1) for i in range(shards)]
    same_core = [[2 * i + c for i in range(chips)] for c in range(2)]
    near = groups([range(h, h + 2) for h in range(0, 12, 2)], [range(4)])
    far = groups([range(l, 12, 2) for l in range(2)], [[y] for y in range(4)])
    shape = jax.ShapeDtypeStruct

    got = lax.ppermute(inputs, "fsdp", swap)
    got_grads = lax.ppermute(grads, "fsdp", swap)

    vmem = pl.BlockSpec(memory_space=pltpu.VMEM)
    part_a, part_b, top, rest = pl.pallas_call(
        functools.partial(front_kernel, factor),
        out_shape=(
            shape((rank, width_k), BF16),
            shape((rank, width_k), BF16),
            shape((rank, tokens), BF16),
            shape((rank, tokens), BF16),
        ),
        in_specs=[pl.BlockSpec(memory_space=pltpu.SMEM), vmem],
        out_specs=(vmem,) * 4,
        cost_estimate=cost(4 * rank * width_k * tokens, 4 * rank * width_k + 2 * tokens * width_k),
        compiler_params=limit(12),
        name="front",
    )(projection_key, grads)

    def whole(a, b):
        return pl.BlockSpec((a, b), lambda i, *_: (0, 0))

    pair = pl.BlockSpec((tokens, rows), lambda i, core: (0, 2 * i + core[0]))
    partial = pl.pallas_call(
        functools.partial(partial_kernel, factor),
        out_shape=shape((chips, rank, rows), BF16),
        grid_spec=pltpu.PrefetchScalarGridSpec(
            num_scalar_prefetch=1,
            grid=(chips,),
            in_specs=[
                pair,
                pair,
                whole(tokens, width_k),
                whole(rank, width_k),
                whole(rank, width_k),
                whole(rank, tokens),
                whole(rank, tokens),
            ],
            out_specs=pl.BlockSpec((1, rank, rows), lambda i, core: (i, 0, 0)),
            scratch_shapes=[pltpu.VMEM((rank, 2 * tokens), BF16)] * 2,
        ),
        cost_estimate=cost(8 * rank * tokens * width // 2, 2 * tokens * width + 2 * rank * rows * chips),
        compiler_params=limit(12),
        name="partial",
    )(core, inputs, got, got_grads, part_a, part_b, top, rest)

    landed = lax.all_to_all(partial, "fsdp", 0, 0, tiled=True, axis_index_groups=same_core)

    side_a, side_b, _ = lax.optimization_barrier((part_a, part_b, partial))
    tile = 128
    local_term, base_momentum, base_anchor = pl.pallas_call(
        functools.partial(side_kernel, unit),
        out_shape=(shape((rank, rows), F32), shape((rows, rank), F32), shape((rows, width_k), F32)),
        grid=(rows // tile,),
        in_specs=[
            pl.BlockSpec((tile, width_k), lambda i: (i, 0)),
            pl.BlockSpec((tile, width_k), lambda i: (i, 0)),
            pl.BlockSpec((tile, rank), lambda i: (i, 0)),
            whole(rank, width_k),
            whole(rank, width_k),
        ],
        out_specs=(
            pl.BlockSpec((rank, tile), lambda i: (0, i)),
            pl.BlockSpec((tile, rank), lambda i: (i, 0)),
            pl.BlockSpec((tile, width_k), lambda i: (i, 0)),
        ),
        cost_estimate=cost(16 * rank * rows * width_k, 10 * rows * width_k + 12 * rows * rank),
        compiler_params=limit(16),
        name="side",
    )(local, anchor, momentum, side_a, side_b)

    mine = (jnp.sum(landed.astype(F32), axis=0) - local_term) * (1.0 / replicas)
    pieces = lax.all_to_all(mine.astype(BF16).reshape(8, rank // 8, rows), "replica", 0, 0, tiled=True, axis_index_groups=near)
    piece = total(pieces)
    sixths = lax.all_to_all(jnp.broadcast_to(piece[None], (6,) + piece.shape), "replica", 0, 0, tiled=True, axis_index_groups=far)
    piece = total(sixths)
    mean = lax.all_to_all(jnp.broadcast_to(piece[None], (8,) + piece.shape), "replica", 0, 0, tiled=True, axis_index_groups=near)

    new_anchor, new_momentum = pl.pallas_call(
        functools.partial(last_kernel, unit),
        out_shape=(shape((rows, width_k), F32), shape((rows, rank), F32)),
        grid=(rows // tile,),
        in_specs=[
            pl.BlockSpec((rank, tile), lambda i: (0, i)),
            pl.BlockSpec((tile, rank), lambda i: (i, 0)),
            pl.BlockSpec((tile, width_k), lambda i: (i, 0)),
            whole(rank, width_k),
            whole(rank, width_k),
        ],
        out_specs=(
            pl.BlockSpec((tile, width_k), lambda i: (i, 0)),
            pl.BlockSpec((tile, rank), lambda i: (i, 0)),
        ),
        cost_estimate=cost(4 * rank * rows * width_k, 8 * rows * width_k + 10 * rows * rank),
        compiler_params=limit(16),
        name="last",
    )(mean.reshape(rank, rows), base_momentum, base_anchor, part_a, part_b)
    return (new_anchor, new_momentum)


def solution(mesh):
    placed = (
        P("replica", "fsdp", None),
        P("replica", "fsdp", None),
        P("replica", "fsdp", None),
        P("fsdp", None),
        P("fsdp", None),
        P(),
    )
    return jax.shard_map(
        on_device,
        mesh=mesh,
        in_specs=placed,
        out_specs=(P("fsdp", None), P("fsdp", None)),
        check_vma=False,
    )
```

time: 147 us -> 111 us (0.76)
  the two profiles are of different devices: /device:TPU:8 before, /device:TPU:10 now
where the time goes in v2:
time: 111 us; the launch traced here: 110 us
  blocking collectives  51.2 us (46%)
  starting transfers between devices  18 us (16%)
  Pallas kernels  15.3 us (14%)
  waiting for transfers between devices  13.8 us (12%)
  local copies, waits for them, and re-layouts  8.67 us (8%)
  other arithmetic  2.18 us (2%)
    all_to_all x1, blocking collectives, on_device(): lax.all_to_all(jnp.broadcast_to(piece[None], (6,) + piece.shape), 'replic...  22.4 us
    all_to_all x1, blocking collectives, on_device(): lax.all_to_all(jnp.broadcast_to(piece[None], (8,) + piece.shape), 'replic...  14.7 us
    all_to_all x1, blocking collectives, on_device(): lax.all_to_all(mine.astype(BF16).reshape(8, rank // 8, rows), 'replica',...  14 us
    all_to_all x1, waiting for transfers between devices, on_device(): lax.all_to_all(partial, 'fsdp', 0, 0, tiled=True, axis_index_groups=same_...  13.7 us
    all_to_all x1, starting transfers between devices, on_device(): lax.all_to_all(partial, 'fsdp', 0, 0, tiled=True, axis_index_groups=same_...  13.6 us
    unnamed x20, local copies, waits for them, and re-layouts  8.63 us
    pallas_call x1, Pallas kernels, on_device(): pl.pallas_call(functools.partial(side_kernel, unit), out_shape=(shape((ra...  6.24 us
    pallas_call x1, Pallas kernels, on_device(): pl.pallas_call(functools.partial(partial_kernel, factor), out_shape=shape...  4.94 us
  transfers between devices with their start and end apart: 3, of which 1 were waited for; matrix products, arithmetic and copies ran while one was open for 0% of the time, Pallas kernels for 7%

profile of v2, /device:TPU:10, one launch (start us, length us, event | category | flops | bytes accessed | tf_op | source)
XLA Modules:
  0.0 109.9 jit_solution(15126695094081831203)
XLA Ops:
  0.6 1.9 %collective-permute-start = (bf16[128,8192]{1,0:T(8,128)(2,1)}, bf16[128,8192]{1,0:T(8,128)(2,1)S(1)}, u32[]{:S(2)}, u32[]{:S(2)}) collective-permute-start(bf16[128,8192]{1,0:T(8,128)(2,1)} %bitcast.6), channel_id=1, source_target_pairs={{0,1},{1,0},{2,3},{3,2},{4,5},{5,4},{6,7},{7,6},{8,9},{9,8},{10,11... | collective-permute-start | bytes 6291464 | tf_op jit(solution)/shard_map/ppermute | solution.py:121
  2.6 2.4 %collective-permute-start.1 = (bf16[128,1024]{1,0:T(8,128)(2,1)}, bf16[128,1024]{1,0:T(8,128)(2,1)S(1)}, u32[]{:S(2)}, u32[]{:S(2)}) collective-permute-start(bf16[128,1024]{1,0:T(8,128)(2,1)} %bitcast.10), channel_id=1, source_target_pairs={{0,1},{1,0},{2,3},{3,2},{4,5},{5,4},{6,7},{7,6},{8,9},{9,8},{10,11... | collective-permute-start | bytes 786440 | tf_op jit(solution)/shard_map/ppermute | solution.py:122
  5.0 0.0 copy-start.8
  5.0 0.9 copy-done.8
  5.9 0.0 copy-start.9
  5.9 0.7 copy-done.9
  6.6 1.4 %front.1 = (bf16[256,1024]{1,0:T(8,128)(2,1)S(1)}, bf16[256,1024]{1,0:T(8,128)(2,1)S(1)}, bf16[256,128]{1,0:T(8,128)(2,1)S(1)}, bf16[256,128]{1,0:T(8,128)(2,1)S(1)}) custom-call(s32[2]{0:T(128)S(1)} %copy-done.9, bf16[128,1024]{1,0:T(8,128)(2,1)S(1)} %bitcast.11), custom_call_target="tpu_custom_call" | custom-call | flops 134217728 | bytes 1310720 | tf_op jit(solution)/shard_map/front/pallas_call | solution.py:125
  8.0 0.0 collective-permute-done.1.gg_ref
  8.0 0.0 collective-permute-done.got_ref
  8.0 0.0 copy-start
  8.0 1.6 %copy-done = bf16[1,128,8192]{2,1,0:T(8,128)(2,1)S(1)} copy-done((bf16[1,128,8192]{2,1,0:T(8,128)(2,1)S(1)}, bf16[1,128,8192]{2,1,0:T(8,128)(2,1)}, u32[]{:S(2)}) %copy-start) | copy-done | bytes 2097176
  9.6 4.9 %partial.1 = bf16[8,256,512]{2,1,0:T(8,128)(2,1)} custom-call(s32[1]{0:T(128)} %bitcast.core_ref, bf16[128,8192]{1,0:T(8,128)(2,1)S(1)} %bitcast.7, bf16[128,8192]{1,0:T(8,128)(2,1)S(1)} %collective-permute-done.got_ref, bf16[128,1024]{1,0:T(8,128)(2,1)S(1)} %collective-permute-done.1.gg_ref, bf16[256,1024]{1,0:T(8,128)(2,1)S(1)} %get-tuple-element.15.a_ref, ...), custom_call_target="tpu_custom_call" | custom-call | flops 1073741824 | bytes 4194304 | tf_op jit(solution)/shard_map/partial/pallas_call | solution.py:144
  14.5 13.6 %all-to-all-start = ((bf16[8,256,512]{2,1,0:T(8,128)(2,1)}), bf16[8,256,512]{2,1,0:T(8,128)(2,1)}, u32[]{:S(2)}, u32[]{:S(2)}) async-start(bf16[8,256,512]{2,1,0:T(8,128)(2,1)} %partial.1), calls=%async_computation | async-start | bytes 4194304 | tf_op jit(solution)/shard_map/all_to_all | solution.py:167
  28.2 0.0 copy-start.5
  28.2 1.6 %copy-done.5 = f32[512,1024]{1,0:T(8,128)S(1)} copy-done((f32[512,1024]{1,0:T(8,128)S(1)}, f32[512,1024]{1,0:T(8,128)}, u32[]{:S(2)}) %copy-start.5) | copy-done | bytes 2097176
  29.8 0.0 copy-start.6
  29.8 1.2 %copy-done.6 = bf16[1,512,1024]{2,1,0:T(8,128)(2,1)S(1)} copy-done((bf16[1,512,1024]{2,1,0:T(8,128)(2,1)S(1)}, bf16[1,512,1024]{2,1,0:T(8,128)(2,1)}, u32[]{:S(2)}) %copy-start.6) | copy-done | bytes 1048600
  31.0 0.0 copy-start.7
  31.0 1.0 copy-done.7
  32.0 6.2 %side.1 = (f32[256,512]{1,0:T(8,128)S(1)}, f32[512,256]{1,0:T(8,128)S(1)}, f32[512,1024]{1,0:T(8,128)S(1)}) custom-call(bf16[512,1024]{1,0:T(8,128)(2,1)S(1)} %bitcast.9, f32[512,1024]{1,0:T(8,128)S(1)} %copy-done.5, f32[512,256]{1,0:T(8,128)S(1)} %copy-done.7, bf16[256,1024]{1,0:T(8,128)(2,1)S(1)} %get-tuple-element.15.a_ref, ...), custom_call_target="tpu_custom_call" | custom-call | flops 2147483648 | bytes 6815744 | tf_op jit(solution)/shard_map/side/pallas_call | solution.py:171
  38.3 0.0 copy-start.1
  38.3 0.8 copy-done.1
  39.1 0.0 copy-start.3
  39.1 0.8 copy-done.3
  39.9 13.7 %all-to-all-done = bf16[8,256,512]{2,1,0:T(8,128)(2,1)} async-done(((bf16[8,256,512]{2,1,0:T(8,128)(2,1)}), bf16[8,256,512]{2,1,0:T(8,128)(2,1)}, u32[]{:S(2)}, u32[]{:S(2)}) %all-to-all-start) | async-done | bytes 2097184 | tf_op jit(solution)/shard_map/all_to_all | solution.py:167
  53.6 0.0 copy-start.4
  53.6 2.0 %convert_reduce_fusion = f32[256,512]{1,0:T(8,128)S(1)} fusion(bf16[8,256,512]{2,1,0:T(8,128)(2,1)} %all-to-all-done), kind=kLoop, calls=%fused_computation | loop fusion | flops 1966080 | bytes 2621440 | tf_op jit(solution)/shard_map/reduce_sum | solution.py:192
  55.6 0.0 copy-start.2
  55.6 0.0 copy-done.4
  55.7 0.1 multiply_convert_fusion
  55.8 14.0 %all_to_all.20 = bf16[8,32,512]{2,1,0:T(8,128)(2,1)S(1)} all-to-all(bf16[8,32,512]{2,1,0:T(8,128)(2,1)S(1)} %bitcast.12), channel_id=1, replica_groups={{0,16,32,48,64,80,96,112},{128,144,160,176,192,208,224,240},{256,272,28..., dimensions={0} | all-to-all | bytes 524288 | tf_op jit(solution)/shard_map/all_to_all | solution.py:193
  69.9 22.4 %all_to_all.21 = bf16[6,32,512]{2,1,0:T(8,128)(2,1)S(1)} all-to-all(bf16[6,32,512]{2,1,0:T(8,128)(2,1)S(1)} %broadcast_in_dim.4), channel_id=1, replica_groups={{0,128,256,384,512,640},{16,144,272,400,528,656},{32,160,288,416,544,67..., dimensions={0} | all-to-all | bytes 393216 | tf_op jit(solution)/shard_map/all_to_all | solution.py:195
  92.4 14.7 %all_to_all.22 = bf16[8,32,512]{2,1,0:T(8,128)(2,1)S(1)} all-to-all(bf16[8,32,512]{2,1,0:T(8,128)(2,1)S(1)} %broadcast_in_dim.5), channel_id=1, replica_groups={{0,16,32,48,64,80,96,112},{128,144,160,176,192,208,224,240},{256,272,28..., dimensions={0} | all-to-all | bytes 524288 | tf_op jit(solution)/shard_map/all_to_all | solution.py:197
  107.1 0.0 copy-done.2
  107.1 2.7 %last.1 = (f32[512,1024]{1,0:T(8,128)}, f32[512,256]{1,0:T(8,128)}) custom-call(bf16[256,512]{1,0:T(8,128)(2,1)S(1)} %bitcast.8, f32[512,256]{1,0:T(8,128)S(1)} %copy-done.2, f32[512,1024]{1,0:T(8,128)S(1)} %get-tuple-element.19.base_anchor_ref, bf16[256,1024]{1,0:T(8,128)(2,1)S(1)} %get-tuple-element.15.a_ref, bf16[256,1024]{1,0:T(8,128)(2,1)S(1)} %get-tuple-element.16.b_ref), custom_call_target="tpu_custom_call" | custom-call | flops 536870912 | bytes 5505024 | tf_op jit(solution)/shard_map/last/pallas_call | solution.py:199
  (6 shorter events, 0.1 us)
Async XLA Ops:
  0.6 7.4 %collective-permute-start = (bf16[128,8192]{1,0:T(8,128)(2,1)}, bf16[128,8192]{1,0:T(8,128)(2,1)S(1)}, u32[]{:S(2)}, u32[]{:S(2)}) collective-permute-start(bf16[128,8192]{1,0:T(8,128)(2,1)} %bitcast.6), channel_id=1, source_target_pairs={{0,1},{1,0},{2,3},{3,2},{4,5},{5,4},{6,7},{7,6},{8,9},{9,8},{10,11... | collective-permute-start | bytes 6291464 | tf_op jit(solution)/shard_map/ppermute | solution.py:121
  2.6 5.4 %collective-permute-start.1 = (bf16[128,1024]{1,0:T(8,128)(2,1)}, bf16[128,1024]{1,0:T(8,128)(2,1)S(1)}, u32[]{:S(2)}, u32[]{:S(2)}) collective-permute-start(bf16[128,1024]{1,0:T(8,128)(2,1)} %bitcast.10), channel_id=1, source_target_pairs={{0,1},{1,0},{2,3},{3,2},{4,5},{5,4},{6,7},{7,6},{8,9},{9,8},{10,11... | collective-permute-start | bytes 786440 | tf_op jit(solution)/shard_map/ppermute | solution.py:122
  5.0 1.0 copy-start.8
  5.9 0.7 copy-start.9
  8.0 1.6 %copy-start = (bf16[1,128,8192]{2,1,0:T(8,128)(2,1)S(1)}, bf16[1,128,8192]{2,1,0:T(8,128)(2,1)}, u32[]{:S(2)}) copy-start(bf16[1,128,8192]{2,1,0:T(8,128)(2,1)} %param.6) | copy-start | bytes 6291460
  14.5 39.1 %all-to-all-start = ((bf16[8,256,512]{2,1,0:T(8,128)(2,1)}), bf16[8,256,512]{2,1,0:T(8,128)(2,1)}, u32[]{:S(2)}, u32[]{:S(2)}) async-start(bf16[8,256,512]{2,1,0:T(8,128)(2,1)} %partial.1), calls=%async_computation | async-start | bytes 4194304 | tf_op jit(solution)/shard_map/all_to_all | solution.py:167
  28.2 1.6 %copy-start.5 = (f32[512,1024]{1,0:T(8,128)S(1)}, f32[512,1024]{1,0:T(8,128)}, u32[]{:S(2)}) copy-start(f32[512,1024]{1,0:T(8,128)} %anchor_ref.1) | copy-start | bytes 6291460
  29.8 1.2 %copy-start.6 = (bf16[1,512,1024]{2,1,0:T(8,128)(2,1)S(1)}, bf16[1,512,1024]{2,1,0:T(8,128)(2,1)}, u32[]{:S(2)}) copy-start(bf16[1,512,1024]{2,1,0:T(8,128)(2,1)} %param.8) | copy-start | bytes 3145732
  31.0 1.0 copy-start.7
  38.3 0.8 copy-start.1
  39.1 0.8 copy-start.3
  53.6 2.0 %copy-start.4 = (f32[256,512]{1,0:T(8,128)S(1)}, f32[256,512]{1,0:T(8,128)}, u32[]{:S(2)}) copy-start(f32[256,512]{1,0:T(8,128)} %copy-done.3) | copy-start | bytes 1572868
  55.6 51.5 %copy-start.2 = (f32[512,256]{1,0:T(8,128)S(1)}, f32[512,256]{1,0:T(8,128)}, u32[]{:S(2)}) copy-start(f32[512,256]{1,0:T(8,128)} %copy-done.1) | copy-start | bytes 1572868

commit v3 on v2

v3 whole, which is shorter than its diff:
```python
import functools

import jax
import jax.numpy as jnp
from jax import lax
from jax.experimental import pallas as pl
from jax.experimental.pallas import tpu as pltpu
from jax.sharding import PartitionSpec as P

F32 = jnp.float32
BF16 = jnp.bfloat16
NN = (((1,), (0,)), ((), ()))
NT = (((1,), (1,)), ((), ()))


def mm(a, b, dims=NN):
    return lax.dot_general(a, b, dims, preferred_element_type=F32)


def split(x):
    top = x.astype(BF16)
    return top, (x - top.astype(F32)).astype(BF16)


def cost(flops, bytes_accessed):
    return pl.CostEstimate(flops=flops, bytes_accessed=bytes_accessed, transcendentals=0)


def front_kernel(factor, key_hbm, grads_hbm, a_ref, b_ref, top_ref, rest_ref, key_ref, grads_ref, sems):
    key_copy = pltpu.make_async_copy(key_hbm, key_ref, sems.at[0])
    grads_copy = pltpu.make_async_copy(grads_hbm, grads_ref, sems.at[1])
    key_copy.start()
    grads_copy.start()
    rank, width_k = a_ref.shape
    step = 256
    r_index = lax.broadcasted_iota(jnp.int32, (rank, step), 0) * 374761393
    k_index = lax.broadcasted_iota(jnp.int32, (rank, step), 1) * 668265261
    base = r_index + k_index
    key_copy.wait()
    start = key_ref[0] + key_ref[1] * 1103515245
    for k in range(0, width_k, step):
        shift = (k * 668265261 + 2**31) % 2**32 - 2**31
        hashed = base + (start + jnp.int32(shift))
        hashed = jnp.bitwise_xor(hashed, lax.shift_right_logical(hashed, jnp.int32(15)))
        hashed = hashed * 739982445
        hashed = jnp.bitwise_xor(hashed, lax.shift_right_logical(hashed, jnp.int32(12)))
        hashed = hashed * 695938361
        hashed = jnp.bitwise_xor(hashed, lax.shift_right_logical(hashed, jnp.int32(15)))
        high = jnp.bitwise_and(lax.shift_right_logical(hashed, jnp.int32(16)), 255).astype(F32)
        low = jnp.bitwise_and(lax.shift_right_logical(hashed, jnp.int32(8)), 255).astype(F32)
        a_ref[:, k : k + step] = ((high - 127.5) * 256.0).astype(BF16)
        b_ref[:, k : k + step] = (low - 127.5).astype(BF16)
    grads_copy.wait()
    grads = grads_ref[...]
    top_ref[...], rest_ref[...] = split(factor * (mm(a_ref[...], grads, NT) + mm(b_ref[...], grads, NT)))


def partial_kernel(factor, own_hbm, got_hbm, gg_hbm, a_ref, b_ref, top_ref, rest_ref, out_hbm, acts, grads, tops, rests, sums, own_sems, got_sems, out_sems, gg_sem):
    chips, both, rows = acts.shape
    tokens = both // 2
    core = lax.rem(lax.axis_index("fsdp"), 2)
    gg_copy = pltpu.make_async_copy(gg_hbm, grads, gg_sem)
    gg_copy.start()
    loads = []
    for i in range(chips):
        columns = pl.ds(pl.multiple_of((2 * i + core) * rows, rows), rows)
        own = pltpu.make_async_copy(own_hbm.at[:, columns], acts.at[i, pl.ds(0, tokens)], own_sems.at[i])
        got = pltpu.make_async_copy(got_hbm.at[:, columns], acts.at[i, pl.ds(tokens, tokens)], got_sems.at[i])
        own.start()
        got.start()
        loads.append((own, got))
    gg_copy.wait()
    block = grads[...]
    top, rest = split(factor * (mm(a_ref[...], block, NT) + mm(b_ref[...], block, NT)))
    tops[:, :tokens] = top_ref[...]
    tops[:, tokens:] = top
    rests[:, :tokens] = rest_ref[...]
    rests[:, tokens:] = rest
    stores = []
    for i in range(chips):
        for load in loads[i]:
            load.wait()
        sums[i] = (mm(tops[...], acts[i]) + mm(rests[...], acts[i])).astype(BF16)
        store = pltpu.make_async_copy(sums.at[i], out_hbm.at[i], out_sems.at[i])
        store.start()
        stores.append(store)
    for store in stores:
        store.wait()


def sum_kernel(portion, landed_hbm, local_hbm, out_ref, landed, local_ref, local_sem, sems):
    chips, rank, rows = landed.shape
    local_copy = pltpu.make_async_copy(local_hbm, local_ref, local_sem)
    local_copy.start()
    loads = []
    parts = 4
    piece = rank // parts
    for p in range(parts):
        span = pl.ds(p * piece, piece)
        load = pltpu.make_async_copy(landed_hbm.at[:, span], landed.at[:, span], sems.at[p])
        load.start()
        loads.append(load)
    local_copy.wait()
    for p in range(parts):
        span = pl.ds(p * piece, piece)
        loads[p].wait()
        added = landed[0, span].astype(F32)
        for i in range(1, chips):
            added += landed[i, span].astype(F32)
        out_ref[span] = ((added - local_ref[span]) * portion).astype(BF16)


def side_kernel(unit, local_ref, anchor_ref, momentum_ref, a_ref, b_ref, local_term_ref, base_momentum_ref, base_anchor_ref):
    part_a, part_b = a_ref[...], b_ref[...]
    local = local_ref[...]
    local_term_ref[...] = unit * (mm(part_a, local, NT) + mm(part_b, local, NT))
    anchor = anchor_ref[...]
    top, rest = split(anchor)
    anchor_term = unit * (mm(top, part_a, NT) + mm(top, part_b, NT) + mm(rest, part_a, NT))
    base = 0.9 * momentum_ref[...] + anchor_term
    base_momentum_ref[...] = base
    top, rest = split(anchor_term + 0.9 * base)
    base_anchor_ref[...] = anchor - (0.7 * unit) * (mm(top, part_a) + mm(top, part_b) + mm(rest, part_a))


def last_kernel(unit, mean_ref, base_momentum_ref, base_anchor_ref, a_ref, b_ref, new_anchor_hbm, new_momentum_ref, outs, sems):
    tile = outs.shape[1]
    stores = []
    for i in range(outs.shape[0]):
        span = pl.ds(i * tile, tile)
        mean = mean_ref[:, span].astype(F32).T
        new_momentum_ref[span] = base_momentum_ref[span] + mean
        narrow = mean.astype(BF16)
        product = mm(narrow, a_ref[...]) + mm(narrow, b_ref[...])
        outs[i] = base_anchor_ref[span] - (0.7 * 1.9 * unit) * product
        store = pltpu.make_async_copy(outs.at[i], new_anchor_hbm.at[span], sems.at[i])
        store.start()
        stores.append(store)
    for store in stores:
        store.wait()


def limit(mib):
    return pltpu.CompilerParams(vmem_limit_bytes=mib << 20)


def total(x):
    return lax.reduce_precision(jnp.sum(x.astype(F32), axis=0), 8, 7).astype(BF16)


def groups(z_of, y_of):
    return [[z * 4 + y for z in zs for y in ys] for zs in z_of for ys in y_of]


def on_device(activations, grad_out, local_weight, anchor, momentum, projection_key):
    inputs, grads, local = activations[0], grad_out[0], local_weight[0]
    tokens, width = inputs.shape
    width_k, rank = grads.shape[1], momentum.shape[1]
    rows = anchor.shape[0]
    replicas, shards = lax.axis_size("replica"), lax.axis_size("fsdp")
    unit = (12.0 / float(rank)) ** 0.5 / 65536.0
    factor = unit * float(tokens * shards) ** (-0.5)
    chips = shards // 2
    swap = [(i, i ^ 1) for i in range(shards)]
    same_core = [[2 * i + c for i in range(chips)] for c in range(2)]
    near = groups([range(h, h + 2) for h in range(0, 12, 2)], [range(4)])
    far = groups([range(l, 12, 2) for l in range(2)], [[y] for y in range(4)])
    shape = jax.ShapeDtypeStruct

    held = pltpu.with_memory_space_constraint(inputs, pltpu.HBM)
    held_grads = pltpu.with_memory_space_constraint(grads, pltpu.HBM)
    held_key = pltpu.with_memory_space_constraint(projection_key, pltpu.HBM)
    got = lax.ppermute(inputs, "fsdp", swap)
    got_grads = lax.ppermute(grads, "fsdp", swap)

    vmem = pl.BlockSpec(memory_space=pltpu.VMEM)
    hbm = pl.BlockSpec(memory_space=pltpu.HBM)
    free = pl.BlockSpec(memory_space=pl.ANY)
    dma = pltpu.SemaphoreType.DMA
    part_a, part_b, top, rest = pl.pallas_call(
        functools.partial(front_kernel, factor),
        out_shape=(
            shape((rank, width_k), BF16),
            shape((rank, width_k), BF16),
            shape((rank, tokens), BF16),
            shape((rank, tokens), BF16),
        ),
        in_specs=[hbm, hbm],
        out_specs=(vmem,) * 4,
        scratch_shapes=[pltpu.SMEM((2,), jnp.int32), pltpu.VMEM((tokens, width_k), BF16), dma((2,))],
        cost_estimate=cost(4 * rank * width_k * tokens, 4 * rank * width_k + 2 * tokens * width_k),
        compiler_params=limit(12),
        name="front",
    )(held_key, held_grads)

    def whole(a, b):
        return pl.BlockSpec((a, b), lambda i, *_: (0, 0))

    partial = pl.pallas_call(
        functools.partial(partial_kernel, factor),
        out_shape=pltpu.HBM((chips, rank, rows), BF16),
        in_specs=[hbm, free, free, vmem, vmem, vmem, vmem],
        out_specs=free,
        scratch_shapes=[
            pltpu.VMEM((chips, 2 * tokens, rows), BF16),
            pltpu.VMEM((tokens, width_k), BF16),
            pltpu.VMEM((rank, 2 * tokens), BF16),
            pltpu.VMEM((rank, 2 * tokens), BF16),
            pltpu.VMEM((chips, rank, rows), BF16),
            dma((chips,)),
            dma((chips,)),
            dma((chips,)),
            dma,
        ],
        cost_estimate=cost(8 * rank * tokens * width // 2, 2 * tokens * width + 2 * rank * rows * chips),
        compiler_params=limit(16),
        name="partial",
    )(held, got, got_grads, part_a, part_b, top, rest)

    landed = lax.all_to_all(partial, "fsdp", 0, 0, tiled=True, axis_index_groups=same_core)

    side_a, side_b, _ = lax.optimization_barrier((part_a, part_b, partial))
    tile = 128
    local_term, base_momentum, base_anchor = pl.pallas_call(
        functools.partial(side_kernel, unit),
        out_shape=(pltpu.HBM((rank, rows), F32), shape((rows, rank), F32), shape((rows, width_k), F32)),
        grid=(rows // tile,),
        in_specs=[
            pl.BlockSpec((tile, width_k), lambda i: (i, 0)),
            pl.BlockSpec((tile, width_k), lambda i: (i, 0)),
            pl.BlockSpec((tile, rank), lambda i: (i, 0)),
            whole(rank, width_k),
            whole(rank, width_k),
        ],
        out_specs=(
            pl.BlockSpec((rank, tile), lambda i: (0, i)),
            pl.BlockSpec((tile, rank), lambda i: (i, 0)),
            pl.BlockSpec((tile, width_k), lambda i: (i, 0)),
        ),
        cost_estimate=cost(16 * rank * rows * width_k, 10 * rows * width_k + 12 * rows * rank),
        compiler_params=limit(16),
        name="side",
    )(local, anchor, momentum, side_a, side_b)

    mine = pl.pallas_call(
        functools.partial(sum_kernel, 1.0 / replicas),
        out_shape=shape((rank, rows), BF16),
        in_specs=[free, hbm],
        out_specs=vmem,
        scratch_shapes=[pltpu.VMEM((chips, rank, rows), BF16), pltpu.VMEM((rank, rows), F32), dma, dma((4,))],
        cost_estimate=cost(chips * rank * rows, 2 * (chips + 3) * rank * rows),
        compiler_params=limit(12),
        name="gather_sum",
    )(landed, pltpu.with_memory_space_constraint(local_term, pltpu.HBM))
    pieces = lax.all_to_all(mine.reshape(8, rank // 8, rows), "replica", 0, 0, tiled=True, axis_index_groups=near)
    piece = total(pieces)
    sixths = lax.all_to_all(jnp.broadcast_to(piece[None], (6,) + piece.shape), "replica", 0, 0, tiled=True, axis_index_groups=far)
    piece = total(sixths)
    mean = lax.all_to_all(jnp.broadcast_to(piece[None], (8,) + piece.shape), "replica", 0, 0, tiled=True, axis_index_groups=near)

    new_anchor, new_momentum = pl.pallas_call(
        functools.partial(last_kernel, unit),
        out_shape=(pltpu.HBM((rows, width_k), F32), shape((rows, rank), F32)),
        in_specs=[vmem] * 5,
        out_specs=(hbm, vmem),
        scratch_shapes=[pltpu.VMEM((rows // tile, tile, width_k), F32), dma((rows // tile,))],
        cost_estimate=cost(4 * rank * rows * width_k, 8 * rows * width_k + 10 * rows * rank),
        compiler_params=limit(16),
        name="last",
    )(mean.reshape(rank, rows), base_momentum, base_anchor, part_a, part_b)
    return (new_anchor, new_momentum)


def solution(mesh):
    placed = (
        P("replica", "fsdp", None),
        P("replica", "fsdp", None),
        P("replica", "fsdp", None),
        P("fsdp", None),
        P("fsdp", None),
        P(),
    )
    return jax.shard_map(
        on_device,
        mesh=mesh,
        in_specs=placed,
        out_specs=(P("fsdp", None), P("fsdp", None)),
        check_vma=False,
    )
```

time: 111 us -> 107 us (0.964)
  local copies, waits for them, and re-layouts: 8.67 us -> 6.04 us
  other arithmetic: 2.18 us -> 0.08 us
  Pallas kernels: 15.3 us -> 16.6 us
    unnamed x20 -> x14, local copies, waits for them, and re-layouts: 8.63 us -> 6.01 us
    reduce_sum x1 -> x0, other arithmetic: 1.99 us -> none  [on_device(): mine = (jnp.sum(landed.astype(F32), axis=0) - local_term) * (1.0 / replicas)]
    all_to_all x1, blocking collectives: 22.4 us -> 23.8 us  [on_device(): lax.all_to_all(jnp.broadcast_to(piece[None], (6,) + piece.shape), 'replic...]
    pallas_call x3 -> x4, Pallas kernels: 13.9 us -> 14.8 us  [the longest x1 6.39 us: on_device(): pl.pallas_call(functools.partial(side_kernel, unit), out_shape=(pltpu.HBM...]
  transfers between devices with their start and end apart: 3 -> 3, of which waited for: 1 -> 2; matrix products, arithmetic and copies ran while one was open for 0% -> 0% of each run, Pallas kernels for 7% -> 8%
where the time goes in v3:
time: 107 us; the launch traced here: 106 us
  blocking collectives  51.8 us (48%)
  starting transfers between devices  17.3 us (16%)
  Pallas kernels  16.6 us (16%)
  waiting for transfers between devices  13.6 us (13%)
  local copies, waits for them, and re-layouts  6.04 us (6%)
    all_to_all x1, blocking collectives, on_device(): lax.all_to_all(jnp.broadcast_to(piece[None], (6,) + piece.shape), 'replic...  23.8 us
    all_to_all x1, blocking collectives, on_device(): lax.all_to_all(mine.reshape(8, rank // 8, rows), 'replica', 0, 0, tiled=T...  14.1 us
    all_to_all x1, blocking collectives, on_device(): lax.all_to_all(jnp.broadcast_to(piece[None], (8,) + piece.shape), 'replic...  13.9 us
    all_to_all x1, waiting for transfers between devices, on_device(): lax.all_to_all(partial, 'fsdp', 0, 0, tiled=True, axis_index_groups=same_...  13.1 us
    all_to_all x1, starting transfers between devices, on_device(): lax.all_to_all(partial, 'fsdp', 0, 0, tiled=True, axis_index_groups=same_...  12.9 us
    pallas_call x1, Pallas kernels, on_device(): pl.pallas_call(functools.partial(side_kernel, unit), out_shape=(pltpu.HBM...  6.39 us
    unnamed x14, local copies, waits for them, and re-layouts  6.01 us
    pallas_call x1, Pallas kernels, on_device(): pl.pallas_call(functools.partial(partial_kernel, factor), out_shape=pltpu...  4.52 us
  transfers between devices with their start and end apart: 3, of which 2 were waited for; matrix products, arithmetic and copies ran while one was open for 0% of the time, Pallas kernels for 8%

profile of v3, /device:TPU:10, one launch (start us, length us, event | category | flops | bytes accessed | tf_op | source)
XLA Modules:
  0.0 106.1 jit_solution(7133385494700651078)
XLA Ops:
  0.6 1.9 %collective-permute-start = (bf16[128,8192]{1,0:T(8,128)(2,1)}, bf16[128,8192]{1,0:T(8,128)(2,1)S(1)}, u32[]{:S(2)}, u32[]{:S(2)}) collective-permute-start(bf16[128,8192]{1,0:T(8,128)(2,1)} %bitcast.8), channel_id=1, source_target_pairs={{0,1},{1,0},{2,3},{3,2},{4,5},{5,4},{6,7},{7,6},{8,9},{9,8},{10,11... | collective-permute-start | bytes 6291464 | tf_op jit(solution)/shard_map/ppermute | solution.py:173
  2.6 2.4 %collective-permute-start.1 = (bf16[128,1024]{1,0:T(8,128)(2,1)}, bf16[128,1024]{1,0:T(8,128)(2,1)S(1)}, u32[]{:S(2)}, u32[]{:S(2)}) collective-permute-start(bf16[128,1024]{1,0:T(8,128)(2,1)} %bitcast.10), channel_id=1, source_target_pairs={{0,1},{1,0},{2,3},{3,2},{4,5},{5,4},{6,7},{7,6},{8,9},{9,8},{10,11... | collective-permute-start | bytes 786440 | tf_op jit(solution)/shard_map/ppermute | solution.py:174
  5.0 1.8 %front.1 = (bf16[256,1024]{1,0:T(8,128)(2,1)S(1)}, bf16[256,1024]{1,0:T(8,128)(2,1)S(1)}, bf16[256,128]{1,0:T(8,128)(2,1)S(1)}, bf16[256,128]{1,0:T(8,128)(2,1)S(1)}) custom-call(s32[2]{0:T(128)} %key_hbm.1, bf16[128,1024]{1,0:T(8,128)(2,1)} %bitcast.11), custom_call_target="tpu_custom_call" | custom-call | flops 134217728 | bytes 1310720 | tf_op jit(solution)/shard_map/front/pallas_call | solution.py:180
  6.8 0.5 collective-permute-done.1.gg_hbm
  7.3 0.0 collective-permute-done.got_hbm
  7.3 4.5 %partial.1 = bf16[8,256,512]{2,1,0:T(8,128)(2,1)} custom-call(bf16[128,8192]{1,0:T(8,128)(2,1)} %bitcast.9, bf16[128,8192]{1,0:T(8,128)(2,1)S(1)} %collective-permute-done.got_hbm, bf16[128,1024]{1,0:T(8,128)(2,1)S(1)} %collective-permute-done.1.gg_hbm, bf16[256,1024]{1,0:T(8,128)(2,1)S(1)} %get-tuple-element.15.a_ref, ...), custom_call_target="tpu_custom_call" | custom-call | flops 1073741824 | bytes 4194304 | tf_op jit(solution)/shard_map/partial/pallas_call | solution.py:199
  11.8 12.9 %all-to-all-start = ((bf16[8,256,512]{2,1,0:T(8,128)(2,1)}), bf16[8,256,512]{2,1,0:T(8,128)(2,1)S(1)}, u32[]{:S(2)}, u32[]{:S(2)}) async-start(bf16[8,256,512]{2,1,0:T(8,128)(2,1)} %partial.1), calls=%async_computation | async-start | bytes 4194304 | tf_op jit(solution)/shard_map/all_to_all | solution.py:220
  24.7 0.0 copy-start.4
  24.7 1.6 %copy-done.4 = f32[512,1024]{1,0:T(8,128)S(1)} copy-done((f32[512,1024]{1,0:T(8,128)S(1)}, f32[512,1024]{1,0:T(8,128)}, u32[]{:S(2)}) %copy-start.4) | copy-done | bytes 2097176
  26.3 0.0 copy-start.5
  26.3 1.2 %copy-done.5 = bf16[1,512,1024]{2,1,0:T(8,128)(2,1)S(1)} copy-done((bf16[1,512,1024]{2,1,0:T(8,128)(2,1)S(1)}, bf16[1,512,1024]{2,1,0:T(8,128)(2,1)}, u32[]{:S(2)}) %copy-start.5) | copy-done | bytes 1048600
  27.6 0.0 copy-start.6
  27.6 1.0 copy-done.6
  28.6 6.4 %side.1 = (f32[256,512]{1,0:T(8,128)}, f32[512,256]{1,0:T(8,128)S(1)}, f32[512,1024]{1,0:T(8,128)S(1)}) custom-call(bf16[512,1024]{1,0:T(8,128)(2,1)S(1)} %bitcast.7, f32[512,1024]{1,0:T(8,128)S(1)} %copy-done.4, f32[512,256]{1,0:T(8,128)S(1)} %copy-done.6, bf16[256,1024]{1,0:T(8,128)(2,1)S(1)} %get-tuple-element.15.a_ref, ...), custom_call_target="tpu_custom_call" | custom-call | flops 2147483648 | bytes 6815744 | tf_op jit(solution)/shard_map/side/pallas_call | solution.py:224
  35.0 0.0 copy-start
  35.0 1.3 %copy-done = f32[512,1024]{1,0:T(8,128)} copy-done((f32[512,1024]{1,0:T(8,128)}, f32[512,1024]{1,0:T(8,128)S(1)}, u32[]{:S(2)}) %copy-start) | copy-done | bytes 2097176
  36.3 0.0 copy-start.2
  36.3 0.8 copy-done.2
  37.1 13.1 %all-to-all-done.landed_hbm = bf16[8,256,512]{2,1,0:T(8,128)(2,1)S(1)} async-done(((bf16[8,256,512]{2,1,0:T(8,128)(2,1)}), bf16[8,256,512]{2,1,0:T(8,128)(2,1)S(1)}, u32[]{:S(2)}, u32[]{:S(2)}) %all-to-all-start) | async-done | bytes 2097184 | tf_op jit(solution)/shard_map/all_to_all | solution.py:220
  50.2 1.4 %gather_sum.1 = bf16[256,512]{1,0:T(8,128)(2,1)S(1)} custom-call(bf16[8,256,512]{2,1,0:T(8,128)(2,1)S(1)} %all-to-all-done.landed_hbm, f32[256,512]{1,0:T(8,128)} %get-tuple-element.17.local_hbm), custom_call_target="tpu_custom_call" | custom-call | flops 1048576 | bytes 2883584 | tf_op jit(solution)/shard_map/gather_sum/pallas_call | solution.py:245
  51.6 0.0 copy-start.1
  51.6 0.0 copy-start.3
  51.7 14.1 %all_to_all.20 = bf16[8,32,512]{2,1,0:T(8,128)(2,1)S(1)} all-to-all(bf16[8,32,512]{2,1,0:T(8,128)(2,1)S(1)} %bitcast.5), channel_id=1, replica_groups={{0,16,32,48,64,80,96,112},{128,144,160,176,192,208,224,240},{256,272,28..., dimensions={0} | all-to-all | bytes 524288 | tf_op jit(solution)/shard_map/all_to_all | solution.py:255
  65.9 23.8 %all_to_all.21 = bf16[6,32,512]{2,1,0:T(8,128)(2,1)S(1)} all-to-all(bf16[6,32,512]{2,1,0:T(8,128)(2,1)S(1)} %broadcast_in_dim.4), channel_id=1, replica_groups={{0,128,256,384,512,640},{16,144,272,400,528,656},{32,160,288,416,544,67..., dimensions={0} | all-to-all | bytes 393216 | tf_op jit(solution)/shard_map/all_to_all | solution.py:257
  89.7 13.9 %all_to_all.22 = bf16[8,32,512]{2,1,0:T(8,128)(2,1)S(1)} all-to-all(bf16[8,32,512]{2,1,0:T(8,128)(2,1)S(1)} %broadcast_in_dim.5), channel_id=1, replica_groups={{0,16,32,48,64,80,96,112},{128,144,160,176,192,208,224,240},{256,272,28..., dimensions={0} | all-to-all | bytes 524288 | tf_op jit(solution)/shard_map/all_to_all | solution.py:259
  103.6 0.0 copy-done.1
  103.6 0.0 copy-done.3
  103.6 2.5 %last.1 = (f32[512,1024]{1,0:T(8,128)}, f32[512,256]{1,0:T(8,128)}) custom-call(bf16[256,512]{1,0:T(8,128)(2,1)S(1)} %bitcast.6, f32[512,256]{1,0:T(8,128)S(1)} %copy-done.3, f32[512,1024]{1,0:T(8,128)S(1)} %copy-done.1, bf16[256,1024]{1,0:T(8,128)(2,1)S(1)} %get-tuple-element.15.a_ref, bf16[256,1024]{1,0:T(8,128)(2,1)S(1)} %get-tuple-element.16.b_ref), custom_call_target="tpu_custom_call" | custom-call | flops 536870912 | bytes 5505024 | tf_op jit(solution)/shard_map/last/pallas_call | solution.py:261
  (6 shorter events, 0.1 us)
Async XLA Ops:
  0.6 6.6 %collective-permute-start = (bf16[128,8192]{1,0:T(8,128)(2,1)}, bf16[128,8192]{1,0:T(8,128)(2,1)S(1)}, u32[]{:S(2)}, u32[]{:S(2)}) collective-permute-start(bf16[128,8192]{1,0:T(8,128)(2,1)} %bitcast.8), channel_id=1, source_target_pairs={{0,1},{1,0},{2,3},{3,2},{4,5},{5,4},{6,7},{7,6},{8,9},{9,8},{10,11... | collective-permute-start | bytes 6291464 | tf_op jit(solution)/shard_map/ppermute | solution.py:173
  2.6 4.7 %collective-permute-start.1 = (bf16[128,1024]{1,0:T(8,128)(2,1)}, bf16[128,1024]{1,0:T(8,128)(2,1)S(1)}, u32[]{:S(2)}, u32[]{:S(2)}) collective-permute-start(bf16[128,1024]{1,0:T(8,128)(2,1)} %bitcast.10), channel_id=1, source_target_pairs={{0,1},{1,0},{2,3},{3,2},{4,5},{5,4},{6,7},{7,6},{8,9},{9,8},{10,11... | collective-permute-start | bytes 786440 | tf_op jit(solution)/shard_map/ppermute | solution.py:174
  11.8 38.4 %all-to-all-start = ((bf16[8,256,512]{2,1,0:T(8,128)(2,1)}), bf16[8,256,512]{2,1,0:T(8,128)(2,1)S(1)}, u32[]{:S(2)}, u32[]{:S(2)}) async-start(bf16[8,256,512]{2,1,0:T(8,128)(2,1)} %partial.1), calls=%async_computation | async-start | bytes 4194304 | tf_op jit(solution)/shard_map/all_to_all | solution.py:220
  24.7 1.6 %copy-start.4 = (f32[512,1024]{1,0:T(8,128)S(1)}, f32[512,1024]{1,0:T(8,128)}, u32[]{:S(2)}) copy-start(f32[512,1024]{1,0:T(8,128)} %anchor_ref.1) | copy-start | bytes 6291460
  26.3 1.2 %copy-start.5 = (bf16[1,512,1024]{2,1,0:T(8,128)(2,1)S(1)}, bf16[1,512,1024]{2,1,0:T(8,128)(2,1)}, u32[]{:S(2)}) copy-start(bf16[1,512,1024]{2,1,0:T(8,128)(2,1)} %param.8) | copy-start | bytes 3145732
  27.6 1.0 copy-start.6
  35.0 1.3 %copy-start = (f32[512,1024]{1,0:T(8,128)}, f32[512,1024]{1,0:T(8,128)S(1)}, u32[]{:S(2)}) copy-start(f32[512,1024]{1,0:T(8,128)S(1)} %get-tuple-element.19.base_anchor_ref) | copy-start | bytes 6291460
  36.3 0.8 copy-start.2
  51.6 52.0 %copy-start.1 = (f32[512,1024]{1,0:T(8,128)S(1)}, f32[512,1024]{1,0:T(8,128)}, u32[]{:S(2)}) copy-start(f32[512,1024]{1,0:T(8,128)} %copy-done) | copy-start | bytes 6291460
  51.6 52.0 %copy-start.3 = (f32[512,256]{1,0:T(8,128)S(1)}, f32[512,256]{1,0:T(8,128)}, u32[]{:S(2)}) copy-start(f32[512,256]{1,0:T(8,128)} %copy-done.2) | copy-start | bytes 1572868

commit v4 on v3

--- a/solution.py
+++ b/solution.py
@@ -55,9 +55,9 @@
     top_ref[...], rest_ref[...] = split(factor * (mm(a_ref[...], grads, NT) + mm(b_ref[...], grads, NT)))
 
 
-def partial_kernel(factor, own_hbm, got_hbm, gg_hbm, a_ref, b_ref, top_ref, rest_ref, out_hbm, acts, grads, tops, rests, sums, own_sems, got_sems, out_sems, gg_sem):
-    chips, both, rows = acts.shape
-    tokens = both // 2
+def partial_kernel(factor, own_hbm, got_hbm, gg_hbm, a_ref, b_ref, top_ref, rest_ref, out_hbm, acts, grads, tops, sums, own_sems, got_sems, out_sems, gg_sem):
+    chips, tokens, rows = acts.shape
+    tokens = tokens // 2
     core = lax.rem(lax.axis_index("fsdp"), 2)
     gg_copy = pltpu.make_async_copy(gg_hbm, grads, gg_sem)
     gg_copy.start()
@@ -70,17 +70,19 @@
         got.start()
         loads.append((own, got))
     gg_copy.wait()
-    block = grads[...]
-    top, rest = split(factor * (mm(a_ref[...], block, NT) + mm(b_ref[...], block, NT)))
-    tops[:, :tokens] = top_ref[...]
-    tops[:, tokens:] = top
-    rests[:, :tokens] = rest_ref[...]
-    rests[:, tokens:] = rest
+    rank = a_ref.shape[0]
+    both = mm(jnp.concatenate([a_ref[...], b_ref[...]], axis=0), grads[...], NT)
+    top, rest = split(factor * (both[:rank] + both[rank:]))
+    tops[:rank, :tokens] = top_ref[...]
+    tops[:rank, tokens:] = top
+    tops[rank:, :tokens] = rest_ref[...]
+    tops[rank:, tokens:] = rest
     stores = []
     for i in range(chips):
         for load in loads[i]:
             load.wait()
-        sums[i] = (mm(tops[...], acts[i]) + mm(rests[...], acts[i])).astype(BF16)
+        product = mm(tops[...], acts[i])
+        sums[i] = (product[:rank] + product[rank:]).astype(BF16)
         store = pltpu.make_async_copy(sums.at[i], out_hbm.at[i], out_sems.at[i])
         store.start()
         stores.append(store)
@@ -163,8 +165,8 @@
     chips = shards // 2
     swap = [(i, i ^ 1) for i in range(shards)]
     same_core = [[2 * i + c for i in range(chips)] for c in range(2)]
-    near = groups([range(h, h + 2) for h in range(0, 12, 2)], [range(4)])
-    far = groups([range(l, 12, 2) for l in range(2)], [[y] for y in range(4)])
+    near = groups([range(h, h + 4) for h in range(0, 12, 4)], [[0, 1], [3, 2]])
+    far = groups([range(l, 12, 4) for l in range(4)], [[0, 3], [1, 2]])
     shape = jax.ShapeDtypeStruct
 
     held = pltpu.with_memory_space_constraint(inputs, pltpu.HBM)
@@ -204,8 +206,7 @@
         scratch_shapes=[
             pltpu.VMEM((chips, 2 * tokens, rows), BF16),
             pltpu.VMEM((tokens, width_k), BF16),
-            pltpu.VMEM((rank, 2 * tokens), BF16),
-            pltpu.VMEM((rank, 2 * tokens), BF16),
+            pltpu.VMEM((2 * rank, 2 * tokens), BF16),
             pltpu.VMEM((chips, rank, rows), BF16),
             dma((chips,)),
             dma((chips,)),

time: 107 us -> 107 us (level)
    all_to_all x1, blocking collectives: 23.8 us -> 26.9 us  [on_device(): lax.all_to_all(jnp.broadcast_to(piece[None], (6,) + piece.shape), 'replic...]
    all_to_all x1, blocking collectives: 13.9 us -> 12.1 us  [on_device(): lax.all_to_all(jnp.broadcast_to(piece[None], (8,) + piece.shape), 'replic...]
    all_to_all x1, blocking collectives: 14.1 us -> 12.8 us  [on_device(): lax.all_to_all(mine.reshape(8, rank // 8, rows), 'replica', 0, 0, tiled=T...]
where the time goes in v4:
time: 107 us; the launch traced here: 106 us
  blocking collectives  51.8 us (48%)
  starting transfers between devices  17.2 us (16%)
  Pallas kernels  16.6 us (16%)
  waiting for transfers between devices  13.6 us (13%)
  local copies, waits for them, and re-layouts  6.04 us (6%)
    all_to_all x1, blocking collectives, on_device(): lax.all_to_all(jnp.broadcast_to(piece[None], (6,) + piece.shape), 'replic...  26.9 us
    all_to_all x1, waiting for transfers between devices, on_device(): lax.all_to_all(partial, 'fsdp', 0, 0, tiled=True, axis_index_groups=same_...  13.1 us
    all_to_all x1, starting transfers between devices, on_device(): lax.all_to_all(partial, 'fsdp', 0, 0, tiled=True, axis_index_groups=same_...  12.9 us
    all_to_all x1, blocking collectives, on_device(): lax.all_to_all(mine.reshape(8, rank // 8, rows), 'replica', 0, 0, tiled=T...  12.8 us
    all_to_all x1, blocking collectives, on_device(): lax.all_to_all(jnp.broadcast_to(piece[None], (8,) + piece.shape), 'replic...  12.1 us
    pallas_call x1, Pallas kernels, on_device(): pl.pallas_call(functools.partial(side_kernel, unit), out_shape=(pltpu.HBM...  6.39 us
    unnamed x14, local copies, waits for them, and re-layouts  6.01 us
    pallas_call x1, Pallas kernels, on_device(): pl.pallas_call(functools.partial(partial_kernel, factor), out_shape=pltpu...  4.48 us
  transfers between devices with their start and end apart: 3, of which 2 were waited for; matrix products, arithmetic and copies ran while one was open for 0% of the time, Pallas kernels for 8%

profile of v4, /device:TPU:10, one launch (start us, length us, event | category | flops | bytes accessed | tf_op | source)
XLA Modules:
  0.0 106.1 jit_solution(9649925394758014392)
XLA Ops:
  0.6 1.9 %collective-permute-start = (bf16[128,8192]{1,0:T(8,128)(2,1)}, bf16[128,8192]{1,0:T(8,128)(2,1)S(1)}, u32[]{:S(2)}, u32[]{:S(2)}) collective-permute-start(bf16[128,8192]{1,0:T(8,128)(2,1)} %bitcast.8), channel_id=1, source_target_pairs={{0,1},{1,0},{2,3},{3,2},{4,5},{5,4},{6,7},{7,6},{8,9},{9,8},{10,11... | collective-permute-start | bytes 6291464 | tf_op jit(solution)/shard_map/ppermute | solution.py:175
  2.6 2.4 %collective-permute-start.1 = (bf16[128,1024]{1,0:T(8,128)(2,1)}, bf16[128,1024]{1,0:T(8,128)(2,1)S(1)}, u32[]{:S(2)}, u32[]{:S(2)}) collective-permute-start(bf16[128,1024]{1,0:T(8,128)(2,1)} %bitcast.10), channel_id=1, source_target_pairs={{0,1},{1,0},{2,3},{3,2},{4,5},{5,4},{6,7},{7,6},{8,9},{9,8},{10,11... | collective-permute-start | bytes 786440 | tf_op jit(solution)/shard_map/ppermute | solution.py:176
  5.0 1.8 %front.1 = (bf16[256,1024]{1,0:T(8,128)(2,1)S(1)}, bf16[256,1024]{1,0:T(8,128)(2,1)S(1)}, bf16[256,128]{1,0:T(8,128)(2,1)S(1)}, bf16[256,128]{1,0:T(8,128)(2,1)S(1)}) custom-call(s32[2]{0:T(128)} %key_hbm.1, bf16[128,1024]{1,0:T(8,128)(2,1)} %bitcast.11), custom_call_target="tpu_custom_call" | custom-call | flops 134217728 | bytes 1310720 | tf_op jit(solution)/shard_map/front/pallas_call | solution.py:182
  6.8 0.5 collective-permute-done.1.gg_hbm
  7.3 0.0 collective-permute-done.got_hbm
  7.3 4.5 %partial.1 = bf16[8,256,512]{2,1,0:T(8,128)(2,1)} custom-call(bf16[128,8192]{1,0:T(8,128)(2,1)} %bitcast.9, bf16[128,8192]{1,0:T(8,128)(2,1)S(1)} %collective-permute-done.got_hbm, bf16[128,1024]{1,0:T(8,128)(2,1)S(1)} %collective-permute-done.1.gg_hbm, bf16[256,1024]{1,0:T(8,128)(2,1)S(1)} %get-tuple-element.15.a_ref, ...), custom_call_target="tpu_custom_call" | custom-call | flops 1073741824 | bytes 4194304 | tf_op jit(solution)/shard_map/partial/pallas_call | solution.py:201
  11.8 12.9 %all-to-all-start = ((bf16[8,256,512]{2,1,0:T(8,128)(2,1)}), bf16[8,256,512]{2,1,0:T(8,128)(2,1)S(1)}, u32[]{:S(2)}, u32[]{:S(2)}) async-start(bf16[8,256,512]{2,1,0:T(8,128)(2,1)} %partial.1), calls=%async_computation | async-start | bytes 4194304 | tf_op jit(solution)/shard_map/all_to_all | solution.py:221
  24.7 0.0 copy-start.4
  24.7 1.6 %copy-done.4 = f32[512,1024]{1,0:T(8,128)S(1)} copy-done((f32[512,1024]{1,0:T(8,128)S(1)}, f32[512,1024]{1,0:T(8,128)}, u32[]{:S(2)}) %copy-start.4) | copy-done | bytes 2097176
  26.3 0.0 copy-start.5
  26.3 1.2 %copy-done.5 = bf16[1,512,1024]{2,1,0:T(8,128)(2,1)S(1)} copy-done((bf16[1,512,1024]{2,1,0:T(8,128)(2,1)S(1)}, bf16[1,512,1024]{2,1,0:T(8,128)(2,1)}, u32[]{:S(2)}) %copy-start.5) | copy-done | bytes 1048600
  27.5 0.0 copy-start.6
  27.5 1.0 copy-done.6
  28.5 6.4 %side.1 = (f32[256,512]{1,0:T(8,128)}, f32[512,256]{1,0:T(8,128)S(1)}, f32[512,1024]{1,0:T(8,128)S(1)}) custom-call(bf16[512,1024]{1,0:T(8,128)(2,1)S(1)} %bitcast.7, f32[512,1024]{1,0:T(8,128)S(1)} %copy-done.4, f32[512,256]{1,0:T(8,128)S(1)} %copy-done.6, bf16[256,1024]{1,0:T(8,128)(2,1)S(1)} %get-tuple-element.15.a_ref, ...), custom_call_target="tpu_custom_call" | custom-call | flops 2147483648 | bytes 6815744 | tf_op jit(solution)/shard_map/side/pallas_call | solution.py:225
  34.9 0.0 copy-start
  34.9 1.3 %copy-done = f32[512,1024]{1,0:T(8,128)} copy-done((f32[512,1024]{1,0:T(8,128)}, f32[512,1024]{1,0:T(8,128)S(1)}, u32[]{:S(2)}) %copy-start) | copy-done | bytes 2097176
  36.3 0.0 copy-start.2
  36.3 0.8 copy-done.2
  37.1 13.1 %all-to-all-done.landed_hbm = bf16[8,256,512]{2,1,0:T(8,128)(2,1)S(1)} async-done(((bf16[8,256,512]{2,1,0:T(8,128)(2,1)}), bf16[8,256,512]{2,1,0:T(8,128)(2,1)S(1)}, u32[]{:S(2)}, u32[]{:S(2)}) %all-to-all-start) | async-done | bytes 2097184 | tf_op jit(solution)/shard_map/all_to_all | solution.py:221
  50.2 1.4 %gather_sum.1 = bf16[256,512]{1,0:T(8,128)(2,1)S(1)} custom-call(bf16[8,256,512]{2,1,0:T(8,128)(2,1)S(1)} %all-to-all-done.landed_hbm, f32[256,512]{1,0:T(8,128)} %get-tuple-element.17.local_hbm), custom_call_target="tpu_custom_call" | custom-call | flops 1048576 | bytes 2883584 | tf_op jit(solution)/shard_map/gather_sum/pallas_call | solution.py:246
  51.6 0.0 copy-start.1
  51.6 0.0 copy-start.3
  51.6 12.8 %all_to_all.20 = bf16[8,32,512]{2,1,0:T(8,128)(2,1)S(1)} all-to-all(bf16[8,32,512]{2,1,0:T(8,128)(2,1)S(1)} %bitcast.5), channel_id=1, replica_groups={{0,16,64,80,128,144,192,208},{48,32,112,96,176,160,240,224},{256,272,32..., dimensions={0} | all-to-all | bytes 524288 | tf_op jit(solution)/shard_map/all_to_all | solution.py:256
  64.6 26.9 %all_to_all.21 = bf16[6,32,512]{2,1,0:T(8,128)(2,1)S(1)} all-to-all(bf16[6,32,512]{2,1,0:T(8,128)(2,1)S(1)} %broadcast_in_dim.4), channel_id=1, replica_groups={{0,48,256,304,512,560},{16,32,272,288,528,544},{64,112,320,368,576,624}..., dimensions={0} | all-to-all | bytes 393216 | tf_op jit(solution)/shard_map/all_to_all | solution.py:258
  91.5 12.1 %all_to_all.22 = bf16[8,32,512]{2,1,0:T(8,128)(2,1)S(1)} all-to-all(bf16[8,32,512]{2,1,0:T(8,128)(2,1)S(1)} %broadcast_in_dim.5), channel_id=1, replica_groups={{0,16,64,80,128,144,192,208},{48,32,112,96,176,160,240,224},{256,272,32..., dimensions={0} | all-to-all | bytes 524288 | tf_op jit(solution)/shard_map/all_to_all | solution.py:260
  103.6 0.0 copy-done.1
  103.6 0.0 copy-done.3
  103.6 2.5 %last.1 = (f32[512,1024]{1,0:T(8,128)}, f32[512,256]{1,0:T(8,128)}) custom-call(bf16[256,512]{1,0:T(8,128)(2,1)S(1)} %bitcast.6, f32[512,256]{1,0:T(8,128)S(1)} %copy-done.3, f32[512,1024]{1,0:T(8,128)S(1)} %copy-done.1, bf16[256,1024]{1,0:T(8,128)(2,1)S(1)} %get-tuple-element.15.a_ref, bf16[256,1024]{1,0:T(8,128)(2,1)S(1)} %get-tuple-element.16.b_ref), custom_call_target="tpu_custom_call" | custom-call | flops 536870912 | bytes 5505024 | tf_op jit(solution)/shard_map/last/pallas_call | solution.py:262
  (6 shorter events, 0.1 us)
Async XLA Ops:
  0.6 6.6 %collective-permute-start = (bf16[128,8192]{1,0:T(8,128)(2,1)}, bf16[128,8192]{1,0:T(8,128)(2,1)S(1)}, u32[]{:S(2)}, u32[]{:S(2)}) collective-permute-start(bf16[128,8192]{1,0:T(8,128)(2,1)} %bitcast.8), channel_id=1, source_target_pairs={{0,1},{1,0},{2,3},{3,2},{4,5},{5,4},{6,7},{7,6},{8,9},{9,8},{10,11... | collective-permute-start | bytes 6291464 | tf_op jit(solution)/shard_map/ppermute | solution.py:175
  2.6 4.7 %collective-permute-start.1 = (bf16[128,1024]{1,0:T(8,128)(2,1)}, bf16[128,1024]{1,0:T(8,128)(2,1)S(1)}, u32[]{:S(2)}, u32[]{:S(2)}) collective-permute-start(bf16[128,1024]{1,0:T(8,128)(2,1)} %bitcast.10), channel_id=1, source_target_pairs={{0,1},{1,0},{2,3},{3,2},{4,5},{5,4},{6,7},{7,6},{8,9},{9,8},{10,11... | collective-permute-start | bytes 786440 | tf_op jit(solution)/shard_map/ppermute | solution.py:176
  11.8 38.4 %all-to-all-start = ((bf16[8,256,512]{2,1,0:T(8,128)(2,1)}), bf16[8,256,512]{2,1,0:T(8,128)(2,1)S(1)}, u32[]{:S(2)}, u32[]{:S(2)}) async-start(bf16[8,256,512]{2,1,0:T(8,128)(2,1)} %partial.1), calls=%async_computation | async-start | bytes 4194304 | tf_op jit(solution)/shard_map/all_to_all | solution.py:221
  24.7 1.6 %copy-start.4 = (f32[512,1024]{1,0:T(8,128)S(1)}, f32[512,1024]{1,0:T(8,128)}, u32[]{:S(2)}) copy-start(f32[512,1024]{1,0:T(8,128)} %anchor_ref.1) | copy-start | bytes 6291460
  26.3 1.2 %copy-start.5 = (bf16[1,512,1024]{2,1,0:T(8,128)(2,1)S(1)}, bf16[1,512,1024]{2,1,0:T(8,128)(2,1)}, u32[]{:S(2)}) copy-start(bf16[1,512,1024]{2,1,0:T(8,128)(2,1)} %param.8) | copy-start | bytes 3145732
  27.5 1.0 copy-start.6
  34.9 1.3 %copy-start = (f32[512,1024]{1,0:T(8,128)}, f32[512,1024]{1,0:T(8,128)S(1)}, u32[]{:S(2)}) copy-start(f32[512,1024]{1,0:T(8,128)S(1)} %get-tuple-element.19.base_anchor_ref) | copy-start | bytes 6291460
  36.3 0.8 copy-start.2
  51.6 52.0 %copy-start.1 = (f32[512,1024]{1,0:T(8,128)S(1)}, f32[512,1024]{1,0:T(8,128)}, u32[]{:S(2)}) copy-start(f32[512,1024]{1,0:T(8,128)} %copy-done) | copy-start | bytes 6291460
  51.6 52.0 %copy-start.3 = (f32[512,256]{1,0:T(8,128)S(1)}, f32[512,256]{1,0:T(8,128)}, u32[]{:S(2)}) copy-start(f32[512,256]{1,0:T(8,128)} %copy-done.2) | copy-start | bytes 1572868

commit v5 on v4

--- a/solution.py
+++ b/solution.py
@@ -26,12 +26,24 @@
     return pl.CostEstimate(flops=flops, bytes_accessed=bytes_accessed, transcendentals=0)
 
 
-def front_kernel(factor, key_hbm, grads_hbm, a_ref, b_ref, top_ref, rest_ref, key_ref, grads_ref, sems):
+def front_kernel(factor, key_hbm, grads_hbm, acts_hbm, a_ref, b_ref, top_ref, rest_ref, pack_hbm, key_ref, grads_ref, pack, sems, give_sems):
     key_copy = pltpu.make_async_copy(key_hbm, key_ref, sems.at[0])
     grads_copy = pltpu.make_async_copy(grads_hbm, grads_ref, sems.at[1])
     key_copy.start()
     grads_copy.start()
     rank, width_k = a_ref.shape
+    tokens, given = grads_ref.shape[0], pack.shape[1] - 2 * rank
+    chips = give_sems.shape[0]
+    rows = given // chips
+    other = 1 - lax.rem(lax.axis_index("fsdp"), 2)
+    gives = []
+    for i in range(chips):
+        columns = pl.ds(pl.multiple_of((2 * i + other) * rows, rows), rows)
+        give = pltpu.make_async_copy(acts_hbm.at[:, columns], pack.at[:, pl.ds(i * rows, rows)], give_sems.at[i])
+        give.start()
+        gives.append(give)
+    acts_out = pltpu.make_async_copy(pack.at[:, pl.ds(0, given)], pack_hbm.at[:, pl.ds(0, given)], sems.at[2])
+    last_out = pltpu.make_async_copy(pack.at[:, pl.ds(given, 2 * rank)], pack_hbm.at[:, pl.ds(given, 2 * rank)], sems.at[3])
     step = 256
     r_index = lax.broadcasted_iota(jnp.int32, (rank, step), 0) * 374761393
     k_index = lax.broadcasted_iota(jnp.int32, (rank, step), 1) * 668265261
@@ -50,33 +62,44 @@
         low = jnp.bitwise_and(lax.shift_right_logical(hashed, jnp.int32(8)), 255).astype(F32)
         a_ref[:, k : k + step] = ((high - 127.5) * 256.0).astype(BF16)
         b_ref[:, k : k + step] = (low - 127.5).astype(BF16)
+        if k == step:
+            for give in gives:
+                give.wait()
+            acts_out.start()
     grads_copy.wait()
     grads = grads_ref[...]
-    top_ref[...], rest_ref[...] = split(factor * (mm(a_ref[...], grads, NT) + mm(b_ref[...], grads, NT)))
-
-
-def partial_kernel(factor, own_hbm, got_hbm, gg_hbm, a_ref, b_ref, top_ref, rest_ref, out_hbm, acts, grads, tops, sums, own_sems, got_sems, out_sems, gg_sem):
-    chips, tokens, rows = acts.shape
-    tokens = tokens // 2
+    top, rest = split(factor * (mm(a_ref[...], grads, NT) + mm(b_ref[...], grads, NT)))
+    top_ref[...] = top
+    rest_ref[...] = rest
+    for j in range(rank // tokens):
+        piece = slice(j * tokens, (j + 1) * tokens)
+        pack[:, given + j * tokens : given + (j + 1) * tokens] = top[piece]
+        pack[:, given + rank + j * tokens : given + rank + (j + 1) * tokens] = rest[piece]
+    last_out.start()
+    acts_out.wait()
+    last_out.wait()
+
+
+def partial_kernel(own_hbm, got_hbm, top_ref, rest_ref, out_hbm, acts, theirs, tops, sums, own_sems, got_sems, out_sems, last_sem):
+    chips, both, rows = acts.shape
+    rank, tokens = top_ref.shape
     core = lax.rem(lax.axis_index("fsdp"), 2)
-    gg_copy = pltpu.make_async_copy(gg_hbm, grads, gg_sem)
-    gg_copy.start()
+    given = chips * rows
+    last = pltpu.make_async_copy(got_hbm.at[:, pl.ds(given, 2 * rank)], theirs, last_sem)
+    last.start()
     loads = []
     for i in range(chips):
         columns = pl.ds(pl.multiple_of((2 * i + core) * rows, rows), rows)
         own = pltpu.make_async_copy(own_hbm.at[:, columns], acts.at[i, pl.ds(0, tokens)], own_sems.at[i])
-        got = pltpu.make_async_copy(got_hbm.at[:, columns], acts.at[i, pl.ds(tokens, tokens)], got_sems.at[i])
+        got = pltpu.make_async_copy(got_hbm.at[:, pl.ds(i * rows, rows)], acts.at[i, pl.ds(tokens, tokens)], got_sems.at[i])
         own.start()
         got.start()
         loads.append((own, got))
-    gg_copy.wait()
-    rank = a_ref.shape[0]
-    both = mm(jnp.concatenate([a_ref[...], b_ref[...]], axis=0), grads[...], NT)
-    top, rest = split(factor * (both[:rank] + both[rank:]))
     tops[:rank, :tokens] = top_ref[...]
-    tops[:rank, tokens:] = top
     tops[rank:, :tokens] = rest_ref[...]
-    tops[rank:, tokens:] = rest
+    last.wait()
+    for j in range(2 * rank // tokens):
+        tops[j * tokens : (j + 1) * tokens, tokens:] = theirs[:, j * tokens : (j + 1) * tokens]
     stores = []
     for i in range(chips):
         for load in loads[i]:
@@ -172,40 +195,47 @@
     held = pltpu.with_memory_space_constraint(inputs, pltpu.HBM)
     held_grads = pltpu.with_memory_space_constraint(grads, pltpu.HBM)
     held_key = pltpu.with_memory_space_constraint(projection_key, pltpu.HBM)
-    got = lax.ppermute(inputs, "fsdp", swap)
-    got_grads = lax.ppermute(grads, "fsdp", swap)
 
     vmem = pl.BlockSpec(memory_space=pltpu.VMEM)
     hbm = pl.BlockSpec(memory_space=pltpu.HBM)
     free = pl.BlockSpec(memory_space=pl.ANY)
     dma = pltpu.SemaphoreType.DMA
-    part_a, part_b, top, rest = pl.pallas_call(
+    packed = rows * chips + 2 * rank
+    part_a, part_b, top, rest, pack = pl.pallas_call(
         functools.partial(front_kernel, factor),
         out_shape=(
             shape((rank, width_k), BF16),
             shape((rank, width_k), BF16),
             shape((rank, tokens), BF16),
             shape((rank, tokens), BF16),
+            pltpu.HBM((tokens, packed), BF16),
         ),
-        in_specs=[hbm, hbm],
-        out_specs=(vmem,) * 4,
-        scratch_shapes=[pltpu.SMEM((2,), jnp.int32), pltpu.VMEM((tokens, width_k), BF16), dma((2,))],
+        in_specs=[hbm, hbm, hbm],
+        out_specs=(vmem,) * 4 + (hbm,),
+        scratch_shapes=[
+            pltpu.SMEM((2,), jnp.int32),
+            pltpu.VMEM((tokens, width_k), BF16),
+            pltpu.VMEM((tokens, packed), BF16),
+            dma((4,)),
+            dma((chips,)),
+        ],
         cost_estimate=cost(4 * rank * width_k * tokens, 4 * rank * width_k + 2 * tokens * width_k),
         compiler_params=limit(12),
         name="front",
-    )(held_key, held_grads)
+    )(held_key, held_grads, held)
+    got = lax.ppermute(pack, "fsdp", swap)
 
     def whole(a, b):
         return pl.BlockSpec((a, b), lambda i, *_: (0, 0))
 
     partial = pl.pallas_call(
-        functools.partial(partial_kernel, factor),
+        partial_kernel,
         out_shape=pltpu.HBM((chips, rank, rows), BF16),
-        in_specs=[hbm, free, free, vmem, vmem, vmem, vmem],
+        in_specs=[hbm, free, vmem, vmem],
         out_specs=free,
         scratch_shapes=[
             pltpu.VMEM((chips, 2 * tokens, rows), BF16),
-            pltpu.VMEM((tokens, width_k), BF16),
+            pltpu.VMEM((tokens, 2 * rank), BF16),
             pltpu.VMEM((2 * rank, 2 * tokens), BF16),
             pltpu.VMEM((chips, rank, rows), BF16),
             dma((chips,)),
@@ -216,7 +246,7 @@
         cost_estimate=cost(8 * rank * tokens * width // 2, 2 * tokens * width + 2 * rank * rows * chips),
         compiler_params=limit(16),
         name="partial",
-    )(held, got, got_grads, part_a, part_b, top, rest)
+    )(held, got, top, rest)
 
     landed = lax.all_to_all(partial, "fsdp", 0, 0, tiled=True, axis_index_groups=same_core)
 

time: 107 us -> 108 us (level)
  waiting for transfers between devices: 13.6 us -> 16 us
  starting transfers between devices: 17.2 us -> 14.9 us
    ppermute x2 -> x1, waiting for transfers between devices: 0.52 us -> 3.02 us  [on_device(): got = lax.ppermute(pack, 'fsdp', swap)]
    ppermute x2 -> x1, starting transfers between devices: 4.33 us -> 1.92 us  [on_device(): got = lax.ppermute(pack, 'fsdp', swap)]
    pallas_call x1, Pallas kernels: 1.77 us -> 2.91 us  [on_device(): pl.pallas_call(functools.partial(front_kernel, factor), out_shape=(shape(...]
  transfers between devices with their start and end apart: 3 -> 2, of which waited for: 2 -> 2; matrix products, arithmetic and copies ran while one was open for 0% -> 0% of each run, Pallas kernels for 8% -> 6%
where the time goes in v5:
time: 108 us; the launch traced here: 107 us
  blocking collectives  51.9 us (48%)
  Pallas kernels  17.4 us (16%)
  waiting for transfers between devices  16 us (15%)
  starting transfers between devices  14.9 us (14%)
  local copies, waits for them, and re-layouts  6.05 us (6%)
    all_to_all x1, blocking collectives, on_device(): lax.all_to_all(jnp.broadcast_to(piece[None], (6,) + piece.shape), 'replic...  27 us
    all_to_all x1, waiting for transfers between devices, on_device(): lax.all_to_all(partial, 'fsdp', 0, 0, tiled=True, axis_index_groups=same_...  13 us
    all_to_all x1, starting transfers between devices, on_device(): lax.all_to_all(partial, 'fsdp', 0, 0, tiled=True, axis_index_groups=same_...  13 us
    all_to_all x1, blocking collectives, on_device(): lax.all_to_all(mine.reshape(8, rank // 8, rows), 'replica', 0, 0, tiled=T...  12.8 us
    all_to_all x1, blocking collectives, on_device(): lax.all_to_all(jnp.broadcast_to(piece[None], (8,) + piece.shape), 'replic...  12 us
    pallas_call x1, Pallas kernels, on_device(): pl.pallas_call(functools.partial(side_kernel, unit), out_shape=(pltpu.HBM...  6.39 us
    unnamed x14, local copies, waits for them, and re-layouts  6.02 us
    pallas_call x1, Pallas kernels, on_device(): pl.pallas_call(partial_kernel, out_shape=pltpu.HBM((chips, rank, rows), B...  4.19 us
  transfers between devices with their start and end apart: 2, of which 2 were waited for; matrix products, arithmetic and copies ran while one was open for 0% of the time, Pallas kernels for 6%

profile of v5, /device:TPU:10, one launch (start us, length us, event | category | flops | bytes accessed | tf_op | source)
XLA Modules:
  0.0 107.0 jit_solution(11837447593460350066)
XLA Ops:
  0.6 2.9 %front.1 = (bf16[256,1024]{1,0:T(8,128)(2,1)S(1)}, bf16[256,1024]{1,0:T(8,128)(2,1)S(1)}, bf16[256,128]{1,0:T(8,128)(2,1)S(1)}, bf16[256,128]{1,0:T(8,128)(2,1)S(1)}, bf16[128,4608]{1,0:T(8,128)(2,1)}) custom-call(s32[2]{0:T(128)} %key_hbm.1, bf16[128,1024]{1,0:T(8,128)(2,1)} %bitcast.10, bf16[128,8192]{1,0:T(8,128)(2,1)} %bitcast.8), custom_call_target="tpu_custom_call" | custom-call | flops 134217728 | bytes 1310720 | tf_op jit(solution)/shard_map/front/pallas_call | solution.py:204
  3.5 1.9 %collective-permute-start = (bf16[128,4608]{1,0:T(8,128)(2,1)}, bf16[128,4608]{1,0:T(8,128)(2,1)S(1)}, u32[]{:S(2)}, u32[]{:S(2)}) collective-permute-start(bf16[128,4608]{1,0:T(8,128)(2,1)} %get-tuple-element.12), channel_id=1, source_target_pairs={{0,1},{1,0},{2,3},{3,2},{4,5},{5,4},{6,7},{7,6},{8,9},{9,8},{10,11... | collective-permute-start | bytes 3538952 | tf_op jit(solution)/shard_map/ppermute | solution.py:226
  5.5 3.0 %collective-permute-done.got_hbm = bf16[128,4608]{1,0:T(8,128)(2,1)S(1)} collective-permute-done((bf16[128,4608]{1,0:T(8,128)(2,1)}, bf16[128,4608]{1,0:T(8,128)(2,1)S(1)}, u32[]{:S(2)}, u32[]{:S(2)}) %collective-permute-start) | collective-permute-done | bytes 1179680 | tf_op jit(solution)/shard_map/ppermute | solution.py:226
  8.5 4.2 %partial.1 = bf16[8,256,512]{2,1,0:T(8,128)(2,1)} custom-call(bf16[128,8192]{1,0:T(8,128)(2,1)} %bitcast.9, bf16[128,4608]{1,0:T(8,128)(2,1)S(1)} %collective-permute-done.got_hbm, bf16[256,128]{1,0:T(8,128)(2,1)S(1)} %get-tuple-element.13.top_ref, bf16[256,128]{1,0:T(8,128)(2,1)S(1)} %get-tuple-element.14.rest_ref), custom_call_target="tpu_custom_call" | custom-call | flops 1073741824 | bytes 4194304 | tf_op jit(solution)/shard_map/partial/pallas_call | solution.py:231
  12.7 13.0 %all-to-all-start = ((bf16[8,256,512]{2,1,0:T(8,128)(2,1)}), bf16[8,256,512]{2,1,0:T(8,128)(2,1)S(1)}, u32[]{:S(2)}, u32[]{:S(2)}) async-start(bf16[8,256,512]{2,1,0:T(8,128)(2,1)} %partial.1), calls=%async_computation | async-start | bytes 4194304 | tf_op jit(solution)/shard_map/all_to_all | solution.py:251
  25.7 0.0 copy-start.4
  25.7 1.6 %copy-done.4 = f32[512,1024]{1,0:T(8,128)S(1)} copy-done((f32[512,1024]{1,0:T(8,128)S(1)}, f32[512,1024]{1,0:T(8,128)}, u32[]{:S(2)}) %copy-start.4) | copy-done | bytes 2097176
  27.3 0.0 copy-start.5
  27.3 1.2 %copy-done.5 = bf16[1,512,1024]{2,1,0:T(8,128)(2,1)S(1)} copy-done((bf16[1,512,1024]{2,1,0:T(8,128)(2,1)S(1)}, bf16[1,512,1024]{2,1,0:T(8,128)(2,1)}, u32[]{:S(2)}) %copy-start.5) | copy-done | bytes 1048600
  28.5 0.0 copy-start.6
  28.5 1.0 copy-done.6
  29.6 6.4 %side.1 = (f32[256,512]{1,0:T(8,128)}, f32[512,256]{1,0:T(8,128)S(1)}, f32[512,1024]{1,0:T(8,128)S(1)}) custom-call(bf16[512,1024]{1,0:T(8,128)(2,1)S(1)} %bitcast.7, f32[512,1024]{1,0:T(8,128)S(1)} %copy-done.4, f32[512,256]{1,0:T(8,128)S(1)} %copy-done.6, bf16[256,1024]{1,0:T(8,128)(2,1)S(1)} %get-tuple-element.17.a_ref, ...), custom_call_target="tpu_custom_call" | custom-call | flops 2147483648 | bytes 6815744 | tf_op jit(solution)/shard_map/side/pallas_call | solution.py:255
  35.9 0.0 copy-start
  35.9 1.4 %copy-done = f32[512,1024]{1,0:T(8,128)} copy-done((f32[512,1024]{1,0:T(8,128)}, f32[512,1024]{1,0:T(8,128)S(1)}, u32[]{:S(2)}) %copy-start) | copy-done | bytes 2097176
  37.3 0.0 copy-start.2
  37.3 0.8 copy-done.2
  38.1 13.0 %all-to-all-done.landed_hbm = bf16[8,256,512]{2,1,0:T(8,128)(2,1)S(1)} async-done(((bf16[8,256,512]{2,1,0:T(8,128)(2,1)}), bf16[8,256,512]{2,1,0:T(8,128)(2,1)S(1)}, u32[]{:S(2)}, u32[]{:S(2)}) %all-to-all-start) | async-done | bytes 2097184 | tf_op jit(solution)/shard_map/all_to_all | solution.py:251
  51.1 1.4 %gather_sum.1 = bf16[256,512]{1,0:T(8,128)(2,1)S(1)} custom-call(bf16[8,256,512]{2,1,0:T(8,128)(2,1)S(1)} %all-to-all-done.landed_hbm, f32[256,512]{1,0:T(8,128)} %get-tuple-element.19.local_hbm), custom_call_target="tpu_custom_call" | custom-call | flops 1048576 | bytes 2883584 | tf_op jit(solution)/shard_map/gather_sum/pallas_call | solution.py:276
  52.5 0.0 copy-start.1
  52.5 0.0 copy-start.3
  52.5 12.8 %all_to_all.20 = bf16[8,32,512]{2,1,0:T(8,128)(2,1)S(1)} all-to-all(bf16[8,32,512]{2,1,0:T(8,128)(2,1)S(1)} %bitcast.5), channel_id=1, replica_groups={{0,16,64,80,128,144,192,208},{48,32,112,96,176,160,240,224},{256,272,32..., dimensions={0} | all-to-all | bytes 524288 | tf_op jit(solution)/shard_map/all_to_all | solution.py:286
  65.5 27.0 %all_to_all.21 = bf16[6,32,512]{2,1,0:T(8,128)(2,1)S(1)} all-to-all(bf16[6,32,512]{2,1,0:T(8,128)(2,1)S(1)} %broadcast_in_dim.4), channel_id=1, replica_groups={{0,48,256,304,512,560},{16,32,272,288,528,544},{64,112,320,368,576,624}..., dimensions={0} | all-to-all | bytes 393216 | tf_op jit(solution)/shard_map/all_to_all | solution.py:288
  92.5 12.0 %all_to_all.22 = bf16[8,32,512]{2,1,0:T(8,128)(2,1)S(1)} all-to-all(bf16[8,32,512]{2,1,0:T(8,128)(2,1)S(1)} %broadcast_in_dim.5), channel_id=1, replica_groups={{0,16,64,80,128,144,192,208},{48,32,112,96,176,160,240,224},{256,272,32..., dimensions={0} | all-to-all | bytes 524288 | tf_op jit(solution)/shard_map/all_to_all | solution.py:290
  104.5 0.0 copy-done.1
  104.5 0.0 copy-done.3
  104.6 2.5 %last.1 = (f32[512,1024]{1,0:T(8,128)}, f32[512,256]{1,0:T(8,128)}) custom-call(bf16[256,512]{1,0:T(8,128)(2,1)S(1)} %bitcast.6, f32[512,256]{1,0:T(8,128)S(1)} %copy-done.3, f32[512,1024]{1,0:T(8,128)S(1)} %copy-done.1, bf16[256,1024]{1,0:T(8,128)(2,1)S(1)} %get-tuple-element.17.a_ref, bf16[256,1024]{1,0:T(8,128)(2,1)S(1)} %get-tuple-element.18.b_ref), custom_call_target="tpu_custom_call" | custom-call | flops 536870912 | bytes 5505024 | tf_op jit(solution)/shard_map/last/pallas_call | solution.py:292
  (6 shorter events, 0.1 us)
Async XLA Ops:
  3.5 5.0 %collective-permute-start = (bf16[128,4608]{1,0:T(8,128)(2,1)}, bf16[128,4608]{1,0:T(8,128)(2,1)S(1)}, u32[]{:S(2)}, u32[]{:S(2)}) collective-permute-start(bf16[128,4608]{1,0:T(8,128)(2,1)} %get-tuple-element.12), channel_id=1, source_target_pairs={{0,1},{1,0},{2,3},{3,2},{4,5},{5,4},{6,7},{7,6},{8,9},{9,8},{10,11... | collective-permute-start | bytes 3538952 | tf_op jit(solution)/shard_map/ppermute | solution.py:226
  12.7 38.4 %all-to-all-start = ((bf16[8,256,512]{2,1,0:T(8,128)(2,1)}), bf16[8,256,512]{2,1,0:T(8,128)(2,1)S(1)}, u32[]{:S(2)}, u32[]{:S(2)}) async-start(bf16[8,256,512]{2,1,0:T(8,128)(2,1)} %partial.1), calls=%async_computation | async-start | bytes 4194304 | tf_op jit(solution)/shard_map/all_to_all | solution.py:251
  25.7 1.6 %copy-start.4 = (f32[512,1024]{1,0:T(8,128)S(1)}, f32[512,1024]{1,0:T(8,128)}, u32[]{:S(2)}) copy-start(f32[512,1024]{1,0:T(8,128)} %anchor_ref.1) | copy-start | bytes 6291460
  27.3 1.2 %copy-start.5 = (bf16[1,512,1024]{2,1,0:T(8,128)(2,1)S(1)}, bf16[1,512,1024]{2,1,0:T(8,128)(2,1)}, u32[]{:S(2)}) copy-start(bf16[1,512,1024]{2,1,0:T(8,128)(2,1)} %param.8) | copy-start | bytes 3145732
  28.5 1.0 copy-start.6
  35.9 1.4 %copy-start = (f32[512,1024]{1,0:T(8,128)}, f32[512,1024]{1,0:T(8,128)S(1)}, u32[]{:S(2)}) copy-start(f32[512,1024]{1,0:T(8,128)S(1)} %get-tuple-element.21.base_anchor_ref) | copy-start | bytes 6291460
  37.3 0.8 copy-start.2
  52.5 52.0 %copy-start.1 = (f32[512,1024]{1,0:T(8,128)S(1)}, f32[512,1024]{1,0:T(8,128)}, u32[]{:S(2)}) copy-start(f32[512,1024]{1,0:T(8,128)} %copy-done) | copy-start | bytes 6291460
  52.5 52.0 %copy-start.3 = (f32[512,256]{1,0:T(8,128)S(1)}, f32[512,256]{1,0:T(8,128)}, u32[]{:S(2)}) copy-start(f32[512,256]{1,0:T(8,128)} %copy-done.2) | copy-start | bytes 1572868

commit v6 on v4

--- a/solution.py
+++ b/solution.py
@@ -26,12 +26,21 @@
     return pl.CostEstimate(flops=flops, bytes_accessed=bytes_accessed, transcendentals=0)
 
 
-def front_kernel(factor, key_hbm, grads_hbm, a_ref, b_ref, top_ref, rest_ref, key_ref, grads_ref, sems):
+def front_kernel(factor, key_hbm, grads_hbm, acts_hbm, a_ref, b_ref, top_ref, rest_ref, own_ref, key_ref, grads_ref, sems, own_sems):
     key_copy = pltpu.make_async_copy(key_hbm, key_ref, sems.at[0])
     grads_copy = pltpu.make_async_copy(grads_hbm, grads_ref, sems.at[1])
     key_copy.start()
     grads_copy.start()
     rank, width_k = a_ref.shape
+    chips = own_sems.shape[0]
+    rows = own_ref.shape[1] // chips
+    core = lax.rem(lax.axis_index("fsdp"), 2)
+    loads = []
+    for i in range(chips):
+        columns = pl.ds(pl.multiple_of((2 * i + core) * rows, rows), rows)
+        load = pltpu.make_async_copy(acts_hbm.at[:, columns], own_ref.at[:, pl.ds(i * rows, rows)], own_sems.at[i])
+        load.start()
+        loads.append(load)
     step = 256
     r_index = lax.broadcasted_iota(jnp.int32, (rank, step), 0) * 374761393
     k_index = lax.broadcasted_iota(jnp.int32, (rank, step), 1) * 668265261
@@ -53,25 +62,15 @@
     grads_copy.wait()
     grads = grads_ref[...]
     top_ref[...], rest_ref[...] = split(factor * (mm(a_ref[...], grads, NT) + mm(b_ref[...], grads, NT)))
-
-
-def partial_kernel(factor, own_hbm, got_hbm, gg_hbm, a_ref, b_ref, top_ref, rest_ref, out_hbm, acts, grads, tops, sums, own_sems, got_sems, out_sems, gg_sem):
-    chips, tokens, rows = acts.shape
-    tokens = tokens // 2
+    for load in loads:
+        load.wait()
+
+
+def partial_kernel(factor, own_ref, got_ref, gg_ref, a_ref, b_ref, top_ref, rest_ref, out_hbm, tops, sums, out_sems):
+    chips, rank, rows = sums.shape
+    tokens = own_ref.shape[0]
     core = lax.rem(lax.axis_index("fsdp"), 2)
-    gg_copy = pltpu.make_async_copy(gg_hbm, grads, gg_sem)
-    gg_copy.start()
-    loads = []
-    for i in range(chips):
-        columns = pl.ds(pl.multiple_of((2 * i + core) * rows, rows), rows)
-        own = pltpu.make_async_copy(own_hbm.at[:, columns], acts.at[i, pl.ds(0, tokens)], own_sems.at[i])
-        got = pltpu.make_async_copy(got_hbm.at[:, columns], acts.at[i, pl.ds(tokens, tokens)], got_sems.at[i])
-        own.start()
-        got.start()
-        loads.append((own, got))
-    gg_copy.wait()
-    rank = a_ref.shape[0]
-    both = mm(jnp.concatenate([a_ref[...], b_ref[...]], axis=0), grads[...], NT)
+    both = mm(jnp.concatenate([a_ref[...], b_ref[...]], axis=0), gg_ref[...], NT)
     top, rest = split(factor * (both[:rank] + both[rank:]))
     tops[:rank, :tokens] = top_ref[...]
     tops[:rank, tokens:] = top
@@ -79,9 +78,9 @@
     tops[rank:, tokens:] = rest
     stores = []
     for i in range(chips):
-        for load in loads[i]:
-            load.wait()
-        product = mm(tops[...], acts[i])
+        columns = pl.ds(pl.multiple_of((2 * i + core) * rows, rows), rows)
+        acts = jnp.concatenate([own_ref[:, i * rows : (i + 1) * rows], got_ref[:, columns]], axis=0)
+        product = mm(tops[...], acts)
         sums[i] = (product[:rank] + product[rank:]).astype(BF16)
         store = pltpu.make_async_copy(sums.at[i], out_hbm.at[i], out_sems.at[i])
         store.start()
@@ -90,26 +89,19 @@
         store.wait()
 
 
-def sum_kernel(portion, landed_hbm, local_hbm, out_ref, landed, local_ref, local_sem, sems):
-    chips, rank, rows = landed.shape
+def sum_kernel(portion, landed_ref, local_hbm, out_ref, local_ref, added_ref, local_sem):
+    chips, rank, rows = landed_ref.shape
     local_copy = pltpu.make_async_copy(local_hbm, local_ref, local_sem)
     local_copy.start()
-    loads = []
-    parts = 4
-    piece = rank // parts
-    for p in range(parts):
-        span = pl.ds(p * piece, piece)
-        load = pltpu.make_async_copy(landed_hbm.at[:, span], landed.at[:, span], sems.at[p])
-        load.start()
-        loads.append(load)
+    step = 64
+    for p in range(0, rank, step):
+        span = pl.ds(p, step)
+        added = landed_ref[0, span].astype(F32)
+        for i in range(1, chips):
+            added += landed_ref[i, span].astype(F32)
+        added_ref[span] = added
     local_copy.wait()
-    for p in range(parts):
-        span = pl.ds(p * piece, piece)
-        loads[p].wait()
-        added = landed[0, span].astype(F32)
-        for i in range(1, chips):
-            added += landed[i, span].astype(F32)
-        out_ref[span] = ((added - local_ref[span]) * portion).astype(BF16)
+    out_ref[...] = ((added_ref[...] - local_ref[...]) * portion).astype(BF16)
 
 
 def side_kernel(unit, local_ref, anchor_ref, momentum_ref, a_ref, b_ref, local_term_ref, base_momentum_ref, base_anchor_ref):
@@ -177,23 +169,23 @@
 
     vmem = pl.BlockSpec(memory_space=pltpu.VMEM)
     hbm = pl.BlockSpec(memory_space=pltpu.HBM)
-    free = pl.BlockSpec(memory_space=pl.ANY)
     dma = pltpu.SemaphoreType.DMA
-    part_a, part_b, top, rest = pl.pallas_call(
+    part_a, part_b, top, rest, own = pl.pallas_call(
         functools.partial(front_kernel, factor),
         out_shape=(
             shape((rank, width_k), BF16),
             shape((rank, width_k), BF16),
             shape((rank, tokens), BF16),
             shape((rank, tokens), BF16),
+            shape((tokens, rows * chips), BF16),
         ),
-        in_specs=[hbm, hbm],
-        out_specs=(vmem,) * 4,
-        scratch_shapes=[pltpu.SMEM((2,), jnp.int32), pltpu.VMEM((tokens, width_k), BF16), dma((2,))],
+        in_specs=[hbm] * 3,
+        out_specs=(vmem,) * 5,
+        scratch_shapes=[pltpu.SMEM((2,), jnp.int32), pltpu.VMEM((tokens, width_k), BF16), dma((2,)), dma((chips,))],
         cost_estimate=cost(4 * rank * width_k * tokens, 4 * rank * width_k + 2 * tokens * width_k),
         compiler_params=limit(12),
         name="front",
-    )(held_key, held_grads)
+    )(held_key, held_grads, held)
 
     def whole(a, b):
         return pl.BlockSpec((a, b), lambda i, *_: (0, 0))
@@ -201,22 +193,17 @@
     partial = pl.pallas_call(
         functools.partial(partial_kernel, factor),
         out_shape=pltpu.HBM((chips, rank, rows), BF16),
-        in_specs=[hbm, free, free, vmem, vmem, vmem, vmem],
-        out_specs=free,
+        in_specs=[vmem] * 7,
+        out_specs=hbm,
         scratch_shapes=[
-            pltpu.VMEM((chips, 2 * tokens, rows), BF16),
-            pltpu.VMEM((tokens, width_k), BF16),
             pltpu.VMEM((2 * rank, 2 * tokens), BF16),
             pltpu.VMEM((chips, rank, rows), BF16),
             dma((chips,)),
-            dma((chips,)),
-            dma((chips,)),
-            dma,
         ],
         cost_estimate=cost(8 * rank * tokens * width // 2, 2 * tokens * width + 2 * rank * rows * chips),
         compiler_params=limit(16),
         name="partial",
-    )(held, got, got_grads, part_a, part_b, top, rest)
+    )(own, got, got_grads, part_a, part_b, top, rest)
 
     landed = lax.all_to_all(partial, "fsdp", 0, 0, tiled=True, axis_index_groups=same_core)
 
@@ -246,9 +233,9 @@
     mine = pl.pallas_call(
         functools.partial(sum_kernel, 1.0 / replicas),
         out_shape=shape((rank, rows), BF16),
-        in_specs=[free, hbm],
+        in_specs=[vmem, hbm],
         out_specs=vmem,
-        scratch_shapes=[pltpu.VMEM((chips, rank, rows), BF16), pltpu.VMEM((rank, rows), F32), dma, dma((4,))],
+        scratch_shapes=[pltpu.VMEM((rank, rows), F32), pltpu.VMEM((rank, rows), F32), dma],
         cost_estimate=cost(chips * rank * rows, 2 * (chips + 3) * rank * rows),
         compiler_params=limit(12),
         name="gather_sum",

time: 107 us -> 105 us (0.981)
  Pallas kernels: 16.6 us -> 14.8 us
    pallas_call x1, Pallas kernels: 4.48 us -> 2.94 us  [on_device(): pl.pallas_call(functools.partial(partial_kernel, factor), out_shape=pltpu...]
where the time goes in v6:
time: 105 us; the launch traced here: 104 us
  blocking collectives  51.9 us (49%)
  starting transfers between devices  17.3 us (16%)
  Pallas kernels  14.8 us (14%)
  waiting for transfers between devices  13.5 us (13%)
  local copies, waits for them, and re-layouts  6.04 us (6%)
    all_to_all x1, blocking collectives, on_device(): lax.all_to_all(jnp.broadcast_to(piece[None], (6,) + piece.shape), 'replic...  27 us
    all_to_all x1, waiting for transfers between devices, on_device(): lax.all_to_all(partial, 'fsdp', 0, 0, tiled=True, axis_index_groups=same_...  13.1 us
    all_to_all x1, starting transfers between devices, on_device(): lax.all_to_all(partial, 'fsdp', 0, 0, tiled=True, axis_index_groups=same_...  12.9 us
    all_to_all x1, blocking collectives, on_device(): lax.all_to_all(mine.reshape(8, rank // 8, rows), 'replica', 0, 0, tiled=T...  12.8 us
    all_to_all x1, blocking collectives, on_device(): lax.all_to_all(jnp.broadcast_to(piece[None], (8,) + piece.shape), 'replic...  12 us
    pallas_call x1, Pallas kernels, on_device(): pl.pallas_call(functools.partial(side_kernel, unit), out_shape=(pltpu.HBM...  6.39 us
    unnamed x14, local copies, waits for them, and re-layouts  6.01 us
    pallas_call x1, Pallas kernels, on_device(): pl.pallas_call(functools.partial(partial_kernel, factor), out_shape=pltpu...  2.94 us
  transfers between devices with their start and end apart: 3, of which 2 were waited for; matrix products, arithmetic and copies ran while one was open for 0% of the time, Pallas kernels for 8%

profile of v6, /device:TPU:10, one launch (start us, length us, event | category | flops | bytes accessed | tf_op | source)
XLA Modules:
  0.0 104.3 jit_solution(2761634536968754846)
XLA Ops:
  0.6 1.9 %collective-permute-start = (bf16[128,8192]{1,0:T(8,128)(2,1)}, bf16[128,8192]{1,0:T(8,128)(2,1)S(1)}, u32[]{:S(2)}, u32[]{:S(2)}) collective-permute-start(bf16[128,8192]{1,0:T(8,128)(2,1)} %bitcast.8), channel_id=1, source_target_pairs={{0,1},{1,0},{2,3},{3,2},{4,5},{5,4},{6,7},{7,6},{8,9},{9,8},{10,11... | collective-permute-start | bytes 6291464 | tf_op jit(solution)/shard_map/ppermute | solution.py:167
  2.6 2.4 %collective-permute-start.1 = (bf16[128,1024]{1,0:T(8,128)(2,1)}, bf16[128,1024]{1,0:T(8,128)(2,1)S(1)}, u32[]{:S(2)}, u32[]{:S(2)}) collective-permute-start(bf16[128,1024]{1,0:T(8,128)(2,1)} %bitcast.10), channel_id=1, source_target_pairs={{0,1},{1,0},{2,3},{3,2},{4,5},{5,4},{6,7},{7,6},{8,9},{9,8},{10,11... | collective-permute-start | bytes 786440 | tf_op jit(solution)/shard_map/ppermute | solution.py:168
  5.0 1.9 %front.1 = (bf16[256,1024]{1,0:T(8,128)(2,1)S(1)}, bf16[256,1024]{1,0:T(8,128)(2,1)S(1)}, bf16[256,128]{1,0:T(8,128)(2,1)S(1)}, bf16[256,128]{1,0:T(8,128)(2,1)S(1)}, bf16[128,4096]{1,0:T(8,128)(2,1)S(1)}) custom-call(s32[2]{0:T(128)} %key_hbm.1, bf16[128,1024]{1,0:T(8,128)(2,1)} %bitcast.11, bf16[128,8192]{1,0:T(8,128)(2,1)} %bitcast.9), custom_call_target="tpu_custom_call" | custom-call | flops 134217728 | bytes 1310720 | tf_op jit(solution)/shard_map/front/pallas_call | solution.py:173
  6.9 0.4 collective-permute-done.1.gg_ref
  7.3 0.0 collective-permute-done.got_ref
  7.3 2.9 %partial.1 = bf16[8,256,512]{2,1,0:T(8,128)(2,1)} custom-call(bf16[128,4096]{1,0:T(8,128)(2,1)S(1)} %get-tuple-element.12.own_ref, bf16[128,8192]{1,0:T(8,128)(2,1)S(1)} %collective-permute-done.got_ref, bf16[128,1024]{1,0:T(8,128)(2,1)S(1)} %collective-permute-done.1.gg_ref, bf16[256,1024]{1,0:T(8,128)(2,1)S(1)} %get-tuple-element.17.a_ref, ...), custom_call_target="tpu_custom_call" | custom-call | flops 1073741824 | bytes 4194304 | tf_op jit(solution)/shard_map/partial/pallas_call | solution.py:193
  10.2 12.9 %all-to-all-start = ((bf16[8,256,512]{2,1,0:T(8,128)(2,1)}), bf16[8,256,512]{2,1,0:T(8,128)(2,1)S(1)}, u32[]{:S(2)}, u32[]{:S(2)}) async-start(bf16[8,256,512]{2,1,0:T(8,128)(2,1)} %partial.1), calls=%async_computation | async-start | bytes 4194304 | tf_op jit(solution)/shard_map/all_to_all | solution.py:208
  23.2 0.0 copy-start.4
  23.2 1.6 %copy-done.4 = f32[512,1024]{1,0:T(8,128)S(1)} copy-done((f32[512,1024]{1,0:T(8,128)S(1)}, f32[512,1024]{1,0:T(8,128)}, u32[]{:S(2)}) %copy-start.4) | copy-done | bytes 2097176
  24.7 0.0 copy-start.5
  24.8 1.2 %copy-done.5 = bf16[1,512,1024]{2,1,0:T(8,128)(2,1)S(1)} copy-done((bf16[1,512,1024]{2,1,0:T(8,128)(2,1)S(1)}, bf16[1,512,1024]{2,1,0:T(8,128)(2,1)}, u32[]{:S(2)}) %copy-start.5) | copy-done | bytes 1048600
  26.0 0.0 copy-start.6
  26.0 1.0 copy-done.6
  27.0 6.4 %side.1 = (f32[256,512]{1,0:T(8,128)}, f32[512,256]{1,0:T(8,128)S(1)}, f32[512,1024]{1,0:T(8,128)S(1)}) custom-call(bf16[512,1024]{1,0:T(8,128)(2,1)S(1)} %bitcast.7, f32[512,1024]{1,0:T(8,128)S(1)} %copy-done.4, f32[512,256]{1,0:T(8,128)S(1)} %copy-done.6, bf16[256,1024]{1,0:T(8,128)(2,1)S(1)} %get-tuple-element.17.a_ref, ...), custom_call_target="tpu_custom_call" | custom-call | flops 2147483648 | bytes 6815744 | tf_op jit(solution)/shard_map/side/pallas_call | solution.py:212
  33.4 0.0 copy-start
  33.4 1.3 %copy-done = f32[512,1024]{1,0:T(8,128)} copy-done((f32[512,1024]{1,0:T(8,128)}, f32[512,1024]{1,0:T(8,128)S(1)}, u32[]{:S(2)}) %copy-start) | copy-done | bytes 2097176
  34.8 0.0 copy-start.2
  34.8 0.8 copy-done.2
  35.6 13.1 %all-to-all-done.landed_ref = bf16[8,256,512]{2,1,0:T(8,128)(2,1)S(1)} async-done(((bf16[8,256,512]{2,1,0:T(8,128)(2,1)}), bf16[8,256,512]{2,1,0:T(8,128)(2,1)S(1)}, u32[]{:S(2)}, u32[]{:S(2)}) %all-to-all-start) | async-done | bytes 2097184 | tf_op jit(solution)/shard_map/all_to_all | solution.py:208
  48.6 1.1 %gather_sum.1 = bf16[256,512]{1,0:T(8,128)(2,1)S(1)} custom-call(bf16[8,256,512]{2,1,0:T(8,128)(2,1)S(1)} %all-to-all-done.landed_ref, f32[256,512]{1,0:T(8,128)} %get-tuple-element.19.local_hbm), custom_call_target="tpu_custom_call" | custom-call | flops 1048576 | bytes 2883584 | tf_op jit(solution)/shard_map/gather_sum/pallas_call | solution.py:233
  49.7 0.0 copy-start.1
  49.8 0.0 copy-start.3
  49.8 12.8 %all_to_all.20 = bf16[8,32,512]{2,1,0:T(8,128)(2,1)S(1)} all-to-all(bf16[8,32,512]{2,1,0:T(8,128)(2,1)S(1)} %bitcast.5), channel_id=1, replica_groups={{0,16,64,80,128,144,192,208},{48,32,112,96,176,160,240,224},{256,272,32..., dimensions={0} | all-to-all | bytes 524288 | tf_op jit(solution)/shard_map/all_to_all | solution.py:243
  62.7 27.0 %all_to_all.21 = bf16[6,32,512]{2,1,0:T(8,128)(2,1)S(1)} all-to-all(bf16[6,32,512]{2,1,0:T(8,128)(2,1)S(1)} %broadcast_in_dim.4), channel_id=1, replica_groups={{0,48,256,304,512,560},{16,32,272,288,528,544},{64,112,320,368,576,624}..., dimensions={0} | all-to-all | bytes 393216 | tf_op jit(solution)/shard_map/all_to_all | solution.py:245
  89.8 12.0 %all_to_all.22 = bf16[8,32,512]{2,1,0:T(8,128)(2,1)S(1)} all-to-all(bf16[8,32,512]{2,1,0:T(8,128)(2,1)S(1)} %broadcast_in_dim.5), channel_id=1, replica_groups={{0,16,64,80,128,144,192,208},{48,32,112,96,176,160,240,224},{256,272,32..., dimensions={0} | all-to-all | bytes 524288 | tf_op jit(solution)/shard_map/all_to_all | solution.py:247
  101.8 0.0 copy-done.1
  101.8 0.0 copy-done.3
  101.8 2.5 %last.1 = (f32[512,1024]{1,0:T(8,128)}, f32[512,256]{1,0:T(8,128)}) custom-call(bf16[256,512]{1,0:T(8,128)(2,1)S(1)} %bitcast.6, f32[512,256]{1,0:T(8,128)S(1)} %copy-done.3, f32[512,1024]{1,0:T(8,128)S(1)} %copy-done.1, bf16[256,1024]{1,0:T(8,128)(2,1)S(1)} %get-tuple-element.17.a_ref, bf16[256,1024]{1,0:T(8,128)(2,1)S(1)} %get-tuple-element.18.b_ref), custom_call_target="tpu_custom_call" | custom-call | flops 536870912 | bytes 5505024 | tf_op jit(solution)/shard_map/last/pallas_call | solution.py:249
  (6 shorter events, 0.1 us)
Async XLA Ops:
  0.6 6.6 %collective-permute-start = (bf16[128,8192]{1,0:T(8,128)(2,1)}, bf16[128,8192]{1,0:T(8,128)(2,1)S(1)}, u32[]{:S(2)}, u32[]{:S(2)}) collective-permute-start(bf16[128,8192]{1,0:T(8,128)(2,1)} %bitcast.8), channel_id=1, source_target_pairs={{0,1},{1,0},{2,3},{3,2},{4,5},{5,4},{6,7},{7,6},{8,9},{9,8},{10,11... | collective-permute-start | bytes 6291464 | tf_op jit(solution)/shard_map/ppermute | solution.py:167
  2.6 4.7 %collective-permute-start.1 = (bf16[128,1024]{1,0:T(8,128)(2,1)}, bf16[128,1024]{1,0:T(8,128)(2,1)S(1)}, u32[]{:S(2)}, u32[]{:S(2)}) collective-permute-start(bf16[128,1024]{1,0:T(8,128)(2,1)} %bitcast.10), channel_id=1, source_target_pairs={{0,1},{1,0},{2,3},{3,2},{4,5},{5,4},{6,7},{7,6},{8,9},{9,8},{10,11... | collective-permute-start | bytes 786440 | tf_op jit(solution)/shard_map/ppermute | solution.py:168
  10.2 38.4 %all-to-all-start = ((bf16[8,256,512]{2,1,0:T(8,128)(2,1)}), bf16[8,256,512]{2,1,0:T(8,128)(2,1)S(1)}, u32[]{:S(2)}, u32[]{:S(2)}) async-start(bf16[8,256,512]{2,1,0:T(8,128)(2,1)} %partial.1), calls=%async_computation | async-start | bytes 4194304 | tf_op jit(solution)/shard_map/all_to_all | solution.py:208
  23.2 1.6 %copy-start.4 = (f32[512,1024]{1,0:T(8,128)S(1)}, f32[512,1024]{1,0:T(8,128)}, u32[]{:S(2)}) copy-start(f32[512,1024]{1,0:T(8,128)} %anchor_ref.1) | copy-start | bytes 6291460
  24.7 1.2 %copy-start.5 = (bf16[1,512,1024]{2,1,0:T(8,128)(2,1)S(1)}, bf16[1,512,1024]{2,1,0:T(8,128)(2,1)}, u32[]{:S(2)}) copy-start(bf16[1,512,1024]{2,1,0:T(8,128)(2,1)} %param.8) | copy-start | bytes 3145732
  26.0 1.0 copy-start.6
  33.4 1.3 %copy-start = (f32[512,1024]{1,0:T(8,128)}, f32[512,1024]{1,0:T(8,128)S(1)}, u32[]{:S(2)}) copy-start(f32[512,1024]{1,0:T(8,128)S(1)} %get-tuple-element.21.base_anchor_ref) | copy-start | bytes 6291460
  34.8 0.8 copy-start.2
  49.7 52.0 %copy-start.1 = (f32[512,1024]{1,0:T(8,128)S(1)}, f32[512,1024]{1,0:T(8,128)}, u32[]{:S(2)}) copy-start(f32[512,1024]{1,0:T(8,128)} %copy-done) | copy-start | bytes 6291460
  49.8 52.0 %copy-start.3 = (f32[512,256]{1,0:T(8,128)S(1)}, f32[512,256]{1,0:T(8,128)}, u32[]{:S(2)}) copy-start(f32[512,256]{1,0:T(8,128)} %copy-done.2) | copy-start | bytes 1572868
